TPU v7x, 32 devices: a whole 2x2x4 slice. The times are simulated.
32 devices in a mesh: dp: 16 (over z, y, x), seq: 2 (over core).
Axes of the slice: x: 2, y: 2, z: 4, core: 2. Of those that a mesh axis runs over, the one named last changes fastest.
Arguments:
- tokens: bfloat16 [32, 1024, 768], P('dp', 'seq'), may hold values from -6 to 6
- ln1_gain: bfloat16 [768], P('dp'), may hold values from 0.5 to 1.5
- ln1_bias: bfloat16 [768], P('dp'), may hold values from -2 to 2
- qkv_weight: bfloat16 [768, 2304], P('dp'), may hold values from -0.21875 to 0.21875
- shift_taps: bfloat16 [4, 768], P(None, 'dp'), may hold values from -3 to 3
- decay_rates: bfloat16 [768], P('dp'), may hold values from 9.727478e-05 to 0.03125
- out_weight: bfloat16 [768, 768], P('dp'), may hold values from -0.0017089844 to 0.0017089844
- ln2_gain: bfloat16 [768], P('dp'), may hold values from 0.5 to 1.5
- ln2_bias: bfloat16 [768], P('dp'), may hold values from -2 to 2
- up_weight: bfloat16 [768, 3072], P('dp'), may hold values from -0.21875 to 0.21875
- down_weight: bfloat16 [3072, 768], P('dp'), may hold values from -0.109375 to 0.109375
- lengths: int32 [32], P('dp'), may hold values from 256 to 1024, as said below
- out_grad: bfloat16 [32, 1024, 768], P('dp', 'seq'), may hold values from -6 to 6
Outputs:
- mixed: bfloat16 [32, 1024, 768], P('dp', 'seq')
- input_grad: float32 [32, 1024, 768], P('dp', 'seq')
- ln1_gain_grad: float32 [768], P('dp')
- ln1_bias_grad: float32 [768], P('dp')
- qkv_weight_grad: float32 [768, 2304], P('dp')
- shift_taps_grad: float32 [4, 768], P(None, 'dp')
- decay_rates_grad: float32 [768], P('dp')
- out_weight_grad: float32 [768, 768], P('dp')
- ln2_gain_grad: float32 [768], P('dp')
- ln2_bias_grad: float32 [768], P('dp')
- up_weight_grad: float32 [768, 3072], P('dp')
- down_weight_grad: float32 [3072, 768], P('dp')
Inputs may be any that keep to these rules, and one draw needn't show every extreme that they name: `lengths`: of the 2 slots of each index of dp one, drawn from the seed, uses all 1024 positions; the others use 1024 // 4 to 1024.
All inputs are finite; a program needn't handle non-finite values.
Results may differ from a plain program's by a relative error of at most 0.0095.
Values may be sent and summed in bfloat16 or wider, within the bound.
A program may use at most 256 MiB of HBM per device.

v0:
```python
import jax
import jax.numpy as jnp
from jax import lax
from jax.sharding import PartitionSpec as P

HEADS = 12
HEAD_DIM = 64


precise = lax.Precision.HIGHEST


def from_behind(value, axis, steps):
    count = lax.axis_size(axis)
    leading, last = (max(0, -steps), min(count, count - steps))
    return lax.ppermute(value, axis, [(source, source + steps) for source in range(leading, last)])


def as_sent(array):

    def short(part):
        return part.astype(jnp.bfloat16) if part.dtype == jnp.float32 else part

    return jax.tree.map(short, array)


def layer_norm(values, norm_gain, offset):
    center = jnp.mean(values, axis=-1, keepdims=True)
    centered = values - center
    spread = jnp.mean(centered * centered, axis=-1, keepdims=True)
    return centered * lax.rsqrt(spread + 1e-05) * norm_gain + offset


def shift_mix(extended, tap_table):
    block_len = extended.shape[-2] - 3
    mixed_sum = tap_table[0] * extended[..., 3 : 3 + block_len, :]
    for lag_step in range(1, 4):
        mixed_sum = (
            mixed_sum
            + tap_table[lag_step] * extended[..., 3 - lag_step : 3 - lag_step + block_len, :]
        )
    return mixed_sum


def factors(queries, key_rows, rate_vector):
    block_len = queries.shape[1]
    rate_grid = rate_vector.reshape(queries.shape[2], -1)
    positions = jnp.arange(block_len, dtype=jnp.float32)[:, None, None]
    decayed = queries * jnp.exp(-rate_grid * positions)
    lifted = key_rows * jnp.exp(rate_grid * positions)
    tail_keys = key_rows * jnp.exp(-rate_grid * (block_len - 1.0 - positions))
    reaching = queries * jnp.exp(-rate_grid * (positions + 1.0))
    carry_decay = jnp.exp(-rate_grid * block_len)
    return (decayed, lifted, tail_keys, reaching, carry_decay)


def outer_sum(left_rows, right_rows):
    return lax.dot_general(
        left_rows, right_rows, (((0,), (0,)), ((), ())), preferred_element_type=jnp.float32
    )


def back_product(grad_rows, weight):
    return lax.dot_general(
        grad_rows, weight, (((1,), (1,)), ((), ())), preferred_element_type=jnp.float32
    )


def local(
    tokens,
    ln1_gain,
    ln1_bias,
    qkv_weight,
    shift_taps,
    decay_rates,
    out_weight,
    ln2_gain,
    ln2_bias,
    up_weight,
    down_weight,
    lengths,
    out_grad,
):
    slot_count, block_len, model_width = tokens.shape
    token_count = slot_count * block_len
    gathered = (
        lax.all_gather(ln1_gain, "dp", axis=0, tiled=True),
        lax.all_gather(ln1_bias, "dp", axis=0, tiled=True),
        lax.all_gather(qkv_weight, "dp", axis=0, tiled=True),
        lax.all_gather(shift_taps, "dp", axis=1, tiled=True),
        lax.all_gather(decay_rates, "dp", axis=0, tiled=True),
        lax.all_gather(out_weight, "dp", axis=0, tiled=True),
        lax.all_gather(ln2_gain, "dp", axis=0, tiled=True),
        lax.all_gather(ln2_bias, "dp", axis=0, tiled=True),
        lax.all_gather(up_weight, "dp", axis=0, tiled=True),
        lax.all_gather(down_weight, "dp", axis=0, tiled=True),
    )
    gain_one = gathered[0].astype(jnp.float32)
    bias_one = gathered[1].astype(jnp.float32)
    tap_table = gathered[3].astype(jnp.float32)
    rate_vector = gathered[4].astype(jnp.float32)
    gain_two = gathered[6].astype(jnp.float32)
    bias_two = gathered[7].astype(jnp.float32)
    qkv_full = gathered[2]
    out_full = gathered[5]
    up_full = gathered[8]
    down_full = gathered[9]
    inputs = tokens.reshape(token_count, model_width).astype(jnp.float32)
    normed_one = layer_norm(inputs, gain_one, bias_one).astype(jnp.bfloat16)
    projected = jnp.dot(normed_one, qkv_full, preferred_element_type=jnp.float32).astype(
        jnp.bfloat16
    )
    projected = projected.reshape(slot_count, block_len, 3 * model_width)
    key_rows = projected[:, :, model_width : 2 * model_width]
    edge_rows = from_behind(key_rows[:, block_len - 3 :], "seq", 1)
    extended = jnp.concatenate([edge_rows, key_rows], axis=1).astype(jnp.float32)
    shifted = shift_mix(extended, tap_table)
    head_shape = (slot_count, block_len, HEADS, HEAD_DIM)
    flat_shape = (slot_count, block_len, model_width)
    head_queries = projected[:, :, :model_width].astype(jnp.float32).reshape(head_shape)
    head_keys = shifted.reshape(head_shape)
    head_values = projected[:, :, 2 * model_width :].reshape(head_shape)
    decayed, lifted, tail_keys, reaching, carry_decay = factors(
        head_queries, head_keys, rate_vector
    )
    decayed_low = decayed.astype(jnp.bfloat16)
    lifted_low = lifted.astype(jnp.bfloat16)
    tail_low = tail_keys.astype(jnp.bfloat16)
    reach_wide = reaching.astype(jnp.bfloat16).astype(jnp.float32)
    position_ids = jnp.arange(block_len)
    causal = position_ids[:, None] >= position_ids[None, :]
    scores = jnp.einsum(
        "bthk,bshk->bhts", decayed_low, lifted_low, preferred_element_type=jnp.float32
    )
    scores_low = jnp.where(causal, scores, 0.0).astype(jnp.bfloat16)
    within = jnp.einsum(
        "bhts,bshv->bthv", scores_low, head_values, preferred_element_type=jnp.float32
    )
    fresh_state = jnp.einsum(
        "bshk,bshv->bhkv", tail_low, head_values, preferred_element_type=jnp.float32
    )
    empty_state = jnp.zeros_like(fresh_state)
    state_in = empty_state
    for relay_turn in range(lax.axis_size("seq") - 1):
        state_in = from_behind(carry_decay[None, :, :, None] * state_in + fresh_state, "seq", 1)
    inter = jnp.einsum("bthk,bhkv->bthv", reach_wide, state_in, precision=precise)
    mixer = (within + inter).reshape(token_count, model_width).astype(jnp.bfloat16)
    resid = inputs + jnp.dot(mixer, out_full, preferred_element_type=jnp.float32)
    normed_two = layer_norm(resid, gain_two, bias_two).astype(jnp.bfloat16)
    hidden_pre = jnp.dot(normed_two, up_full, preferred_element_type=jnp.float32)
    hidden = jax.nn.gelu(hidden_pre).astype(jnp.bfloat16)
    result = resid + jnp.dot(hidden, down_full, preferred_element_type=jnp.float32)
    mixed = result.reshape(flat_shape).astype(jnp.bfloat16)
    qkv_full, out_full, up_full, down_full = (
        lax.all_gather(qkv_weight, "dp", axis=0, tiled=True),
        lax.all_gather(out_weight, "dp", axis=0, tiled=True),
        lax.all_gather(up_weight, "dp", axis=0, tiled=True),
        lax.all_gather(down_weight, "dp", axis=0, tiled=True),
    )
    positions = lax.axis_index("seq") * block_len + jnp.arange(block_len, dtype=jnp.int32)
    keep_mask = (positions[None, :] < lengths[:, None]).astype(jnp.float32)
    grad_rows = (out_grad.astype(jnp.float32) * keep_mask[:, :, None]).reshape(
        token_count, model_width
    )
    grad_low = grad_rows.astype(jnp.bfloat16)
    down_grad = outer_sum(hidden, grad_low)
    hidden_grad = back_product(grad_low, down_full)
    _, gelu_back = jax.vjp(jax.nn.gelu, hidden_pre)
    pre_grad = gelu_back(hidden_grad)[0].astype(jnp.bfloat16)
    up_grad = outer_sum(normed_two, pre_grad)
    _, norm_two_back = jax.vjp(layer_norm, resid, gain_two, bias_two)
    resid_part, gain_two_grad, bias_two_grad = norm_two_back(back_product(pre_grad, up_full))
    resid_grad = grad_rows + resid_part
    branch_grad = resid_grad.astype(jnp.bfloat16)
    proj_grad = outer_sum(mixer, branch_grad)
    mixer_low = back_product(branch_grad, out_full).astype(jnp.bfloat16).reshape(head_shape)
    mixer_wide = mixer_low.astype(jnp.float32)
    local_grad = jnp.einsum("bthk,bthv->bhkv", reach_wide, mixer_wide, precision=precise)
    state_grad = empty_state
    for relay_turn in range(lax.axis_size("seq") - 1):
        state_grad = from_behind(
            as_sent(carry_decay[None, :, :, None] * state_grad + local_grad), "seq", -1
        )
    score_grad = jnp.einsum(
        "bthv,bshv->bhts", mixer_low, head_values, preferred_element_type=jnp.float32
    ).astype(jnp.bfloat16)
    score_grad = jnp.where(causal, score_grad, jnp.zeros_like(score_grad))
    decayed_grad = jnp.einsum(
        "bhts,bshk->bthk", score_grad, lifted_low, preferred_element_type=jnp.float32
    )
    lifted_grad = jnp.einsum(
        "bhts,bthk->bshk", score_grad, decayed_low, preferred_element_type=jnp.float32
    )
    value_grad = jnp.einsum(
        "bhts,bthv->bshv", scores_low, mixer_low, preferred_element_type=jnp.float32
    )
    value_grad = value_grad + jnp.einsum(
        "bshk,bhkv->bshv", tail_low.astype(jnp.float32), state_grad, precision=precise
    )
    tail_grad = jnp.einsum(
        "bshv,bhkv->bshk", head_values.astype(jnp.float32), state_grad, precision=precise
    )
    reach_grad = jnp.einsum("bthv,bhkv->bthk", mixer_wide, state_in, precision=precise)
    carry_grad = jnp.sum(state_grad * state_in, axis=(0, 3))
    _, factor_back = jax.vjp(factors, head_queries, head_keys, rate_vector)
    query_grad, key_grad, rate_grad = factor_back(
        (decayed_grad, lifted_grad, tail_grad, reach_grad, carry_grad)
    )
    _, shift_back = jax.vjp(shift_mix, extended, tap_table)
    extended_grad, taps_grad = shift_back(key_grad.reshape(flat_shape))
    spill = from_behind(extended_grad[:, :3], "seq", -1)
    keys_grad = jnp.concatenate(
        [extended_grad[:, 3:block_len], extended_grad[:, block_len:] + spill], axis=1
    )
    qkv_grad_low = jnp.concatenate(
        [query_grad.reshape(flat_shape), keys_grad, value_grad.reshape(flat_shape)], axis=2
    )
    qkv_grad_low = qkv_grad_low.reshape(token_count, 3 * model_width).astype(jnp.bfloat16)
    qkv_grad = outer_sum(normed_one, qkv_grad_low)
    _, norm_one_back = jax.vjp(layer_norm, inputs, gain_one, bias_one)
    input_part, gain_one_grad, bias_one_grad = norm_one_back(back_product(qkv_grad_low, qkv_full))
    input_grad = (resid_grad + input_part).reshape(flat_shape)
    reduced = (
        lax.psum_scatter(gain_one_grad, "dp", scatter_dimension=0, tiled=True),
        lax.psum_scatter(bias_one_grad, "dp", scatter_dimension=0, tiled=True),
        lax.psum_scatter(qkv_grad, "dp", scatter_dimension=0, tiled=True),
        lax.psum_scatter(taps_grad, "dp", scatter_dimension=1, tiled=True),
        lax.psum_scatter(rate_grad, "dp", scatter_dimension=0, tiled=True),
        lax.psum_scatter(proj_grad, "dp", scatter_dimension=0, tiled=True),
        lax.psum_scatter(gain_two_grad, "dp", scatter_dimension=0, tiled=True),
        lax.psum_scatter(bias_two_grad, "dp", scatter_dimension=0, tiled=True),
        lax.psum_scatter(up_grad, "dp", scatter_dimension=0, tiled=True),
        lax.psum_scatter(down_grad, "dp", scatter_dimension=0, tiled=True),
    )
    summed = lax.psum(
        (
            reduced[0],
            reduced[1],
            reduced[2],
            reduced[3],
            reduced[4],
            reduced[5],
            reduced[6],
            reduced[7],
            reduced[8],
            reduced[9],
        ),
        "seq",
    )
    return (
        mixed,
        input_grad,
        summed[0],
        summed[1],
        summed[2],
        summed[3],
        summed[4],
        summed[5],
        summed[6],
        summed[7],
        summed[8],
        summed[9],
    )


def solution(mesh):
    in_specs = (
        P("dp", "seq", None),
        P("dp"),
        P("dp"),
        P("dp", None),
        P(None, "dp"),
        P("dp"),
        P("dp", None),
        P("dp"),
        P("dp"),
        P("dp", None),
        P("dp", None),
        P("dp"),
        P("dp", "seq", None),
    )
    out_specs = (
        P("dp", "seq", None),
        P("dp", "seq", None),
        P("dp"),
        P("dp"),
        P("dp", None),
        P(None, "dp"),
        P("dp"),
        P("dp", None),
        P("dp"),
        P("dp"),
        P("dp", None),
        P("dp", None),
    )
    return jax.shard_map(local, mesh=mesh, in_specs=in_specs, out_specs=out_specs, check_vma=False)
```

profile of v0, /device:TPU:0, one launch (start us, length us, event | category | flops | bytes accessed | tf_op | source)
XLA Modules:
  0.0 1185.9 jit_solution(13013981385271929959)
XLA Ops:
  14.9 79.4 %all-reduce.21 = (bf16[768]{0:T(1024)(128)(2,1)S(1)}, bf16[768]{0:T(1024)(128)(2,1)S(1)}, bf16[768]{0:T(1024)(128)(2,1)S(1)}, bf16[768]{0:T(1024)(128)(2,1)S(1)}, bf16[768]{0:T(1024)(128)(2,1)S(1)}) all-reduce(bf16[768]{0:T(1024)(128)(2,1)S(1)} %dynamic-update-slice.1, ...), channel_id=1, replica_groups=mesh['dp'=16,'seq'=2] {'dp'}, use_global_device_ids=true, to_apply=%add.9 | all-reduce | flops 3840 | bytes 15360
  94.4 35.5 %all-gather = bf16[16,48,4]{1,2,0:T(4,128)(2,1)S(1)} all-gather(bf16[1,48,4]{1,2,0:T(4,128)(2,1)S(1)} %bitcast.170), channel_id=1, replica_groups=mesh['dp'=16,'seq'=2] {'dp'}, dimensions={0}, use_global_device_ids=true | all-gather | bytes 6528 | tf_op jit(solution)/shard_map/all_gather | solution.py:90
  170.1 12.0 %select_convert_fusion = bf16[2,12,512,512]{3,2,1,0:T(8,128)(2,1)} fusion(pred[512,512]{1,0:T(8,128)(4,1)S(1)} %iota_compare_fusion, f32[2,512,12,64]{1,3,2,0:T(8,128)} %bitcast.133, f32[512,12,64]{0,2,1:T(8,128)} %get-tuple-element.67, f32[2,512,12,64]{1,3,2,0:T(8,128)} %bitcast.139, f32[512,12,64]{0,2,1:T(8,128)} %multiply_exponential_fusion.2), kind=kOutput, calls=%fused_computation | convolution fusion | flops 821035008 | bytes 22282240 | tf_op jit(solution)/shard_map/bthk,bshk->bhts/dot_general | solution.py:132
  182.1 9.1 fusion.55
  203.2 22.1 %all-gather.10.cloned.1.call-done = bf16[768,3072]{1,0:T(8,128)(2,1)} async-done(((bf16[48,3072]{1,0:T(8,128)(2,1)}), bf16[768,3072]{1,0:T(8,128)(2,1)}) %all-gather.10.cloned.1.call-update) | async-done | bytes 4718608 | tf_op jit(solution)/shard_map/all_gather | solution.py:95
  225.4 11.3 fusion.48
  236.6 70.5 %all-gather.12.cloned.1.call-done = bf16[3072,768]{1,0:T(8,128)(2,1)} async-done(((bf16[192,768]{1,0:T(8,128)(2,1)}), bf16[3072,768]{1,0:T(8,128)(2,1)}) %all-gather.12.cloned.1.call-update) | async-done | bytes 4718608 | tf_op jit(solution)/shard_map/all_gather | solution.py:96
  307.1 15.5 %fusion.6 = bf16[1024,3072]{1,0:T(8,128)(2,1)S(1)} fusion(f32[1024,3072]{1,0:T(8,128)} %fusion.48, bf16[1024,768]{1,0:T(8,128)(2,1)} %bitcast_convert_fusion, bf16[3072,768]{1,0:T(8,128)(2,1)} %all-gather.12.cloned.1.call-done), kind=kOutput, calls=%fused_computation.9 | convolution fusion | flops 4894752768 | bytes 25165824 | tf_op jit(solution)/shard_map/dot_general | solution.py:64
  322.6 10.8 multiply_reduce_fusion
  355.8 8.0 convert_select_fusion
  363.9 8.6 fusion.44
  372.4 11.6 fusion.45
  385.4 9.0 fusion.30
  428.9 9.2 fusion.25
  440.0 10.6 fusion.47
  450.7 12.9 %fusion.49 = f32[3072,768]{1,0:T(8,128)} fusion(bf16[1024,768]{1,0:T(8,128)(2,1)} %bitcast_convert_fusion, f32[1024,3072]{1,0:T(8,128)} %fusion.48), kind=kOutput, calls=%fused_computation.134 | convolution fusion | flops 4860149760 | bytes 23592960 | tf_op jit(solution)/shard_map/dot_general | solution.py:58
  464.3 12.9 %add_convert_fusion.1 = bf16[1024,768]{1,0:T(8,128)(2,1)} fusion(f32[1024,768]{1,0:T(8,128)S(1)} %copy-done.16, bf16[3072,768]{1,0:T(8,128)(2,1)} %all-gather.12.cloned.1.call-done, f32[1024,3072]{1,0:T(8,128)} %fusion.48), kind=kOutput, calls=%fused_computation.59 | convolution fusion | flops 4861722624 | bytes 22020096 | tf_op jit(solution)/shard_map/dot_general | solution.py:152
  485.3 28.9 %reduce-scatter.10.cloned.1.call-done = f32[48,768]{1,0:T(8,128)} async-done(((f32[768,768]{1,0:T(8,128)}), f32[48,768]{1,0:T(8,128)}) %reduce-scatter.10.cloned.1.call-update) | async-done | bytes 147472 | tf_op jit(solution)/shard_map/reduce_scatter | solution.py:229
  514.1 156.5 %reduce-scatter.8.cloned.1.call-done = f32[48,2304]{1,0:T(8,128)} async-done(((f32[768,2304]{1,0:T(8,128)}), f32[48,2304]{1,0:T(8,128)}) %reduce-scatter.8.cloned.1.call-update) | async-done | bytes 442384 | tf_op jit(solution)/shard_map/reduce_scatter | solution.py:226
  670.6 176.7 %reduce-scatter.12.cloned.1.call-done = f32[48,3072]{1,0:T(8,128)} async-done(((f32[768,3072]{1,0:T(8,128)}), f32[48,3072]{1,0:T(8,128)}) %reduce-scatter.12.cloned.1.call-update) | async-done | bytes 589840 | tf_op jit(solution)/shard_map/reduce_scatter | solution.py:232
  847.3 175.6 %reduce-scatter.14.cloned.1.call-done = f32[192,768]{1,0:T(8,128)} async-done(((f32[3072,768]{1,0:T(8,128)}), f32[192,768]{1,0:T(8,128)}) %reduce-scatter.14.cloned.1.call-update) | async-done | bytes 589840 | tf_op jit(solution)/shard_map/reduce_scatter | solution.py:233
  1033.7 74.8 %all-reduce.18 = (f32[768]{0:T(1024)S(1)}, f32[768]{0:T(1024)S(1)}, f32[768]{0:T(1024)S(1)}, f32[768]{0:T(1024)S(1)}, f32[768]{0:T(1024)S(1)}) all-reduce(f32[768]{0:T(1024)S(1)} %get-tuple-element.18, f32[768]{0:T(1024)S(1)} %get-tuple-element.25, f32[768]{0:T(1024)S(1)} %add_add_fusion.4, ...), channel_id=2, replica_groups=mesh['dp'=16,'seq'=2] {'dp'}, use_global_device_ids=true, to_apply=%region_9.10.clone | all-reduce | flops 3840 | bytes 30720
  1113.4 35.6 %reduce-scatter.16.cloned.1.call-done = f32[48,4]{1,0:T(8,128)} async-done(((f32[768,4]{1,0:T(8,128)}), f32[48,4]{1,0:T(8,128)}) %reduce-scatter.16.cloned.1.call-update) | async-done | bytes 784
  1152.9 18.5 %all-reduce.24.cloned.1.call-done = (f32[48,2304]{1,0:T(8,128)}, f32[48,768]{1,0:T(8,128)}, f32[48,3072]{1,0:T(8,128)}, f32[192,768]{1,0:T(8,128)}) async-done(((f32[48,2304]{1,0:T(8,128)}, f32[48,768]{1,0:T(8,128)}, f32[48,3072]{1,0:T(8,128)}, f32[192,768]{1,0:T(8,128)}), (f32[48,2304]{1,0:T(8,128)}, f32[48,768]{1,0:T(8,128)}, f32[48,3072]{1,0:T(8,128)}, ...) | async-done | bytes 1769488 | tf_op jit(solution)/shard_map/psum | solution.py:235
  (260 shorter events, 153.6 us)
Async XLA Ops:
  7.3 87.1 %copy-start.53 = (bf16[4,48]{1,0:T(4,128)(2,1)S(1)}, bf16[4,48]{1,0:T(4,128)(2,1)}, u32[]{:S(2)}) copy-start(bf16[4,48]{1,0:T(4,128)(2,1)} %param.17) | copy-start | bytes 1156
  7.3 122.8 %copy-start.54 = (s32[2]{0:T(128)S(1)}, s32[2]{0:T(128)}, u32[]{:S(2)}) copy-start(s32[2]{0:T(128)} %param.24) | copy-start | bytes 28
  7.3 133.5 %all-gather.6.cloned.1.call-start = ((), (), s32[]{:S(2)}) async-start(), calls=%async_computation.5 | async-start | bytes 3760128 | tf_op jit(solution)/shard_map/all_gather | solution.py:89
  8.0 189.1 %all-gather.8.cloned.1.call-start = ((), (), s32[]{:S(2)}) async-start(), calls=%async_computation.6 | async-start | bytes 1253376 | tf_op jit(solution)/shard_map/all_gather | solution.py:92
  8.8 216.6 %all-gather.10.cloned.1.call-start = ((), (), s32[]{:S(2)}) async-start(), calls=%async_computation.7 | async-start | bytes 5013504 | tf_op jit(solution)/shard_map/all_gather | solution.py:95
  9.5 297.6 %all-gather.12.cloned.1.call-start = ((), (), s32[]{:S(2)}) async-start(), calls=%async_computation.8 | async-start | bytes 5013504 | tf_op jit(solution)/shard_map/all_gather | solution.py:96
  10.1 504.1 %reduce-scatter.10.cloned.1.call-start = ((), (), s32[]{:S(2)}) async-start(), calls=%async_computation.10 | async-start | bytes 2506752 | tf_op jit(solution)/shard_map/reduce_scatter | solution.py:229
  94.3 35.7 %copy-start.48 = (bf16[768]{0:T(1024)(128)(2,1)}, bf16[768]{0:T(1024)(128)(2,1)S(1)}, u32[]{:S(2)}) copy-start(bf16[768]{0:T(1024)(128)(2,1)S(1)} %get-tuple-element.51) | copy-start | bytes 4612
  94.4 37.4 %copy-start.32 = (f32[12,64]{1,0:T(8,128)}, f32[12,64]{1,0:T(8,128)S(1)}, u32[]{:S(2)}) copy-start(f32[12,64]{1,0:T(8,128)S(1)} %reshape.282) | copy-start | bytes 9220
  146.9 8.4 collective-permute-start
  167.8 23.5 %collective-permute-start.1 = (f32[2,12,64,64]{3,2,1,0:T(8,128)}, f32[2,12,64,64]{3,2,1,0:T(8,128)}, u32[]{:S(2)}, u32[]{:S(2)}) collective-permute-start(f32[2,12,64,64]{3,2,1,0:T(8,128)} %convolution_add_fusion.1), channel_id=1, source_target_pairs={{0,1},{2,3},{4,5},{6,7},{8,9},{10,11},{12,13},{14,15},{16,17},{18,... | collective-permute-start | bytes 1179656 | tf_op jit(solution)/shard_map/ppermute | solution.py:16
  384.0 20.1 %collective-permute-start.2 = (bf16[2,12,64,64]{3,2,1,0:T(8,128)(2,1)}, bf16[2,12,64,64]{3,2,1,0:T(8,128)(2,1)}, u32[]{:S(2)}, u32[]{:S(2)}) collective-permute-start(bf16[2,12,64,64]{3,2,1,0:T(8,128)(2,1)} %fusion.29), channel_id=1, source_target_pairs={{1,0},{3,2},{5,4},{7,6},{9,8},{11,10},{13,12},{15,14},{17,16},{19,... | collective-permute-start | bytes 589832 | tf_op jit(solution)/shard_map/ppermute | solution.py:16
  385.3 285.3 %reduce-scatter.8.cloned.1.call-start = ((), (), s32[]{:S(2)}) async-start(), calls=%async_computation.9 | async-start | bytes 7520256 | tf_op jit(solution)/shard_map/reduce_scatter | solution.py:226
  417.2 9.6 collective-permute-start.3
  438.1 409.2 %reduce-scatter.12.cloned.1.call-start = ((), (), s32[]{:S(2)}) async-start(), calls=%async_computation.11 | async-start | bytes 10027008 | tf_op jit(solution)/shard_map/reduce_scatter | solution.py:232
  450.6 572.2 %reduce-scatter.14.cloned.1.call-start = ((), (), s32[]{:S(2)}) async-start(), calls=%async_computation.12 | async-start | bytes 10027008 | tf_op jit(solution)/shard_map/reduce_scatter | solution.py:233
  463.6 685.5 %reduce-scatter.16.cloned.1.call-start = ((), (), s32[]{:S(2)}) async-start(), calls=%async_computation.13 | async-start | bytes 417792
  464.3 16.5 %copy-start.35 = (f32[12,64]{1,0:T(8,128)S(1)}, f32[12,64]{1,0:T(8,128)}, u32[]{:S(2)}) copy-start(f32[12,64]{1,0:T(8,128)} %copy-done.34) | copy-start | bytes 9220
  464.3 16.5 %copy-start.45 = (f32[512]{0:T(512)S(1)}, f32[512]{0:T(512)}, u32[]{:S(2)}) copy-start(f32[512]{0:T(512)} %copy-done.44) | copy-start | bytes 6148
  464.3 16.5 %copy-start.47 = (f32[512]{0:T(512)S(1)}, f32[512]{0:T(512)}, u32[]{:S(2)}) copy-start(f32[512]{0:T(512)} %copy-done.46) | copy-start | bytes 6148
  480.8 542.0 %copy-start.11 = (bf16[2,512,768]{2,1,0:T(8,128)(2,1)S(1)}, bf16[2,512,768]{2,1,0:T(8,128)(2,1)}, u32[]{:S(2)}) copy-start(bf16[2,512,768]{2,1,0:T(8,128)(2,1)} %param.13) | copy-start | bytes 4718596
  480.8 542.0 %copy-start.37 = (f32[768]{0:T(1024)S(1)}, f32[768]{0:T(1024)}, u32[]{:S(2)}) copy-start(f32[768]{0:T(1024)} %copy-done.36) | copy-start | bytes 9220
  480.8 542.0 %copy-start.39 = (f32[1,4,2,128]{3,1,2,0:T(4,128)S(1)}, f32[1,4,2,128]{3,1,2,0:T(4,128)}, u32[]{:S(2)}) copy-start(f32[1,4,2,128]{3,1,2,0:T(4,128)} %copy-done.38) | copy-start | bytes 12292
  485.2 686.2 %all-reduce.24.cloned.1.call-start = ((), (), s32[]{:S(2)}) async-start(), calls=%async_computation.14 | async-start | bytes 3538944 | tf_op jit(solution)/shard_map/psum | solution.py:235
  (50 other events, 302.2 us)
Sparse Core Ops, SparseCore 0:
  10.9 74.7 all-gather.5
  88.5 54.6 all-gather.7
  146.0 79.3 all-gather.9
  228.0 79.0 all-gather.11
  385.5 128.6 reduce-scatter.9
  520.2 150.3 reduce-scatter.7
  677.2 169.9 reduce-scatter.11
  852.9 169.8 reduce-scatter.13
  1028.8 120.2 reduce-scatter.15
  1151.5 19.9 all-reduce.23
where the time goes:
time: 1190 us
  waiting for transfers between devices  687 us (58%)
  blocking collectives  193 us (16%)
  matrix products  192 us (16%)
  local copies, waits for them, and re-layouts  52.4 us (4%)
  other arithmetic  38.3 us (3%)
  between operations  16.9 us (1%)
    reduce_scatter x1, waiting for transfers between devices, local(): lax.psum_scatter(up_grad, 'dp', scatter_dimension=0, tiled=True)  177 us
    reduce_scatter x1, waiting for transfers between devices, local(): lax.psum_scatter(down_grad, 'dp', scatter_dimension=0, tiled=True)  176 us
    reduce_scatter x1, waiting for transfers between devices, local(): lax.psum_scatter(qkv_grad, 'dp', scatter_dimension=0, tiled=True)  156 us
    unnamed x2, blocking collectives  154 us
    all_gather x1, waiting for transfers between devices, local(): lax.all_gather(down_weight, 'dp', axis=0, tiled=True)  70.5 us
    dot_general x4, matrix products, back_product(): lax.dot_general(grad_rows, weight, (((1,), (1,)), ((), ())), preferred_el...  38.6 us
    unnamed x11, waiting for transfers between devices  38.3 us
    dot_general x4, matrix products, outer_sum(): lax.dot_general(left_rows, right_rows, (((0,), (0,)), ((), ())), preferre...  35.5 us
  transfers between devices with their start and end apart: 14, of which 8 were waited for; matrix products, arithmetic and copies ran while one was open for 16% of the time, Pallas kernels for 0%

commit v1 on v0

--- a/solution.py
+++ b/solution.py
@@ -1,13 +1,972 @@
+import functools
+
 import jax
 import jax.numpy as jnp
 from jax import lax
+from jax.experimental import pallas as pl
+from jax.experimental.pallas import tpu as pltpu
 from jax.sharding import PartitionSpec as P
 
 HEADS = 12
 HEAD_DIM = 64
+MESH = pl.DeviceIdType.MESH
+MIB = 2**20
 
 
 precise = lax.Precision.HIGHEST
+
+
+class Place:
+    def __init__(self):
+        self.dp = lax.axis_index("dp")
+        self.core = lax.axis_index("seq")
+        self.z = self.dp // 4
+        self.stride_a = 2 - self.core
+        self.stride_b = 1 + self.core
+        self.a = (self.dp // self.stride_a) % 2
+        self.b = (self.dp // self.stride_b) % 2
+
+    def block(self, dz, da, db):
+        z = (self.z + dz) % 4
+        a = (self.a + da) % 2
+        b = (self.b + db) % 2
+        return z * 4 + a * self.stride_a + b * self.stride_b
+
+    def peer(self, dz, da, db):
+        return (self.block(dz, da, db), self.core)
+
+    def sibling(self):
+        return (self.dp, 1 - self.core)
+
+
+PEERS = ((1, 0, 0), (2, 0, 0), (3, 0, 0), (0, 1, 0), (0, 0, 1))
+
+
+def enter(place):
+    barrier = pltpu.get_barrier_semaphore()
+    for step in PEERS:
+        pl.semaphore_signal(barrier, inc=1, device_id=place.peer(*step), device_id_type=MESH)
+    pl.semaphore_signal(barrier, inc=1, device_id=place.sibling(), device_id_type=MESH)
+    pl.semaphore_wait(barrier, len(PEERS) + 1)
+
+
+def index_of(dz, da, db):
+    return dz * 4 + da * 2 + db
+
+
+def gather_kernel(count, *refs):
+    shards, wholes = refs[: count + 1], refs[count + 1 : 2 * count + 2]
+    local_sem, send_sem, pass_sem, recv_sem, other_sem = refs[2 * count + 2 :]
+    place = Place()
+    core = place.core
+    enter(place)
+    started = []
+
+    def half(ref, rows, start):
+        columns = ref.shape[1] // 2
+        return ref.at[
+            pl.ds(pl.multiple_of(start, 16), rows), pl.ds(pl.multiple_of(core * columns, 128), columns)
+        ]
+
+    def window(which, block):
+        if which == count:
+            return wholes[which].at[block]
+        rows = shards[which].shape[0]
+        return half(wholes[which], rows, block * rows)
+
+    def own(which):
+        if which == count:
+            return shards[which].at[...]
+        return half(shards[which], shards[which].shape[0], 0)
+
+    def send(which, what, step, slot):
+        block = place.block(*what)
+        source = own(which) if index_of(*what) == 0 else window(which, block)
+        lands = tuple((w - s) % n for w, s, n in zip(what, step, (4, 2, 2)))
+        copy = pltpu.make_async_remote_copy(
+            src_ref=source,
+            dst_ref=window(which, block),
+            send_sem=send_sem.at[which, slot],
+            recv_sem=recv_sem.at[which, index_of(*lands)],
+            device_id=place.peer(*step),
+            device_id_type=MESH,
+        )
+        copy.start()
+        started.append(copy)
+
+    def wait_block(which, what):
+        block = window(which, place.block(*what))
+        pltpu.make_async_copy(block, block, recv_sem.at[which, index_of(*what)]).wait()
+
+    def pass_on(which, what):
+        if which == count:
+            return
+        block = window(which, place.block(*what))
+        copy = pltpu.make_async_remote_copy(
+            src_ref=block,
+            dst_ref=block,
+            send_sem=pass_sem.at[which, index_of(*what)],
+            recv_sem=other_sem.at[which, index_of(*what)],
+            device_id=place.sibling(),
+            device_id_type=MESH,
+        )
+        copy.start()
+        started.append(copy)
+
+    stays = []
+    for which in range(count + 1):
+        rows = shards[which].shape[0]
+        target = (
+            wholes[which].at[place.dp]
+            if which == count
+            else wholes[which].at[pl.ds(pl.multiple_of(place.dp * rows, 16), rows)]
+        )
+        copy = pltpu.make_async_copy(shards[which], target, local_sem.at[which])
+        copy.start()
+        stays.append(copy)
+    order = (count,) + tuple(range(count))
+    for which in order:
+        for dz in range(1, 4):
+            send(which, (0, 0, 0), (dz, 0, 0), dz)
+        send(which, (0, 0, 0), (0, 1, 0), 4)
+        send(which, (0, 0, 0), (0, 0, 1), 8)
+    for turn in range(len(order) + 2):
+        if turn < len(order):
+            which = order[turn]
+            for dz in range(1, 4):
+                wait_block(which, (dz, 0, 0))
+                send(which, (dz, 0, 0), (0, 1, 0), 4 + dz)
+                send(which, (dz, 0, 0), (0, 0, 1), 8 + dz)
+                pass_on(which, (dz, 0, 0))
+        if 1 <= turn < len(order) + 1:
+            which = order[turn - 1]
+            for dz in range(4):
+                wait_block(which, (dz, 1, 0))
+                send(which, (dz, 1, 0), (0, 0, 1), 12 + dz)
+                pass_on(which, (dz, 1, 0))
+        if 2 <= turn:
+            which = order[turn - 2]
+            for da in range(2):
+                for dz in range(4):
+                    wait_block(which, (dz, da, 1))
+                    pass_on(which, (dz, da, 1))
+    for copy in started:
+        copy.wait_send()
+    for copy in stays:
+        copy.wait()
+    for which in range(count):
+        rows, columns = shards[which].shape
+        for dz in range(4):
+            for da in range(2):
+                for db in range(2):
+                    if index_of(dz, da, db) == 0:
+                        continue
+                    block = (
+                        (place.z + dz) % 4 * 4
+                        + (place.b + da) % 2 * place.stride_b
+                        + (place.a + db) % 2 * place.stride_a
+                    )
+                    arrived = wholes[which].at[
+                        pl.ds(pl.multiple_of(block * rows, 16), rows),
+                        pl.ds(pl.multiple_of((1 - core) * (columns // 2), 128), columns // 2),
+                    ]
+                    pltpu.make_async_copy(
+                        arrived, arrived, other_sem.at[which, index_of(dz, da, db)]
+                    ).wait()
+
+
+def gather_blocks(matrices, small):
+    count = len(matrices)
+    operands = (*matrices, small)
+    shapes = [
+        jax.ShapeDtypeStruct((16 * m.shape[0], m.shape[1]), m.dtype) for m in matrices
+    ] + [jax.ShapeDtypeStruct((16, *small.shape), small.dtype)]
+    dma = pltpu.SemaphoreType.DMA
+    return pl.pallas_call(
+        functools.partial(gather_kernel, count),
+        out_shape=shapes,
+        in_specs=[pl.BlockSpec(memory_space=pltpu.HBM)] * (count + 1),
+        out_specs=[pl.BlockSpec(memory_space=pltpu.HBM)] * (count + 1),
+        scratch_shapes=[
+            dma((count + 1,)),
+            dma((count + 1, 16)),
+            dma((count + 1, 16)),
+            dma((count + 1, 16)),
+            dma((count + 1, 16)),
+        ],
+        compiler_params=pltpu.CompilerParams(collective_id=0, has_side_effects=True),
+        name="gather_weights",
+    )(*operands)
+
+
+def reduce_kernel(count, *refs):
+    grads, small = refs[:count], refs[count]
+    outs, small_out = refs[count + 1 : 2 * count + 1], refs[2 * count + 1]
+    refs = refs[2 * count + 2 :]
+    from_core, merged, from_b, from_a, from_z = (refs[k * count : (k + 1) * count] for k in range(5))
+    small_sums, small_from, send_sem, recv_sem, small_send, small_recv = refs[5 * count :]
+    place = Place()
+    core = place.core
+    enter(place)
+    started = []
+
+    def send(which, stage, source, target, device):
+        copy = pltpu.make_async_remote_copy(
+            src_ref=source,
+            dst_ref=target,
+            send_sem=send_sem.at[which, stage],
+            recv_sem=recv_sem.at[which, stage],
+            device_id=device,
+            device_id_type=MESH,
+        )
+        copy.start()
+        started.append(copy)
+        return copy
+
+    def half(which, side):
+        columns = grads[which].shape[1] // 2
+        return pl.ds(pl.multiple_of(side * columns, 128), columns)
+
+    def rows_of(which, block):
+        rows = grads[which].shape[0] // 16
+        return pl.ds(pl.multiple_of(block * rows, 16), rows)
+
+    def to_sibling(which):
+        return send(
+            which, 0, grads[which].at[:, half(which, 1 - core)], from_core[which], place.sibling()
+        )
+
+    def merge_cores(which, copy):
+        copy.wait_recv()
+        mine = half(which, core)
+
+        def one(block, carry):
+            z, b, a = block // 4, (block // place.stride_b) % 2, (block // place.stride_a) % 2
+            rows = rows_of(which, block)
+            total = grads[which][rows, mine].astype(jnp.float32)
+            total = total + from_core[which][rows].astype(jnp.float32)
+            merged[which][b, a, z] = total.astype(jnp.bfloat16)
+            return carry
+
+        lax.fori_loop(0, 16, one, 0)
+        return send(which, 1, merged[which].at[1 - place.b], from_b[which], place.peer(0, 0, 1))
+
+    def merge_b(which, copy):
+        copy.wait_recv()
+
+        def one(block, carry):
+            a, z = block // 4, block % 4
+            total = merged[which][place.b, a, z].astype(jnp.float32)
+            total = total + from_b[which][a, z].astype(jnp.float32)
+            from_b[which][a, z] = total.astype(jnp.bfloat16)
+            return carry
+
+        lax.fori_loop(0, 8, one, 0)
+        return send(which, 2, from_b[which].at[1 - place.a], from_a[which], place.peer(0, 1, 0))
+
+    def merge_a(which, copy):
+        copy.wait_recv()
+
+        def one(z, carry):
+            total = from_b[which][place.a, z].astype(jnp.float32)
+            total = total + from_a[which][z].astype(jnp.float32)
+            from_a[which][z] = total.astype(jnp.bfloat16)
+            return carry
+
+        lax.fori_loop(0, 4, one, 0)
+        return [
+            send(
+                which,
+                2 + dz,
+                from_a[which].at[(place.z + dz) % 4],
+                from_z[which].at[dz - 1],
+                place.peer(dz, 0, 0),
+            )
+            for dz in range(1, 4)
+        ]
+
+    def finish(which, copies):
+        for copy in copies:
+            copy.wait_recv()
+        total = from_a[which][place.z].astype(jnp.float32)
+        for slot in range(3):
+            total = total + from_z[which][slot].astype(jnp.float32)
+        mine = half(which, core)
+        outs[which][:, mine] = total
+        window = outs[which].at[:, mine]
+        return send(which, 6, window, window, place.sibling())
+
+    def send_small(slot, source, target, device):
+        copy = pltpu.make_async_remote_copy(
+            src_ref=source,
+            dst_ref=target,
+            send_sem=small_send.at[slot],
+            recv_sem=small_recv.at[slot],
+            device_id=device,
+            device_id_type=MESH,
+        )
+        copy.start()
+        started.append(copy)
+        return copy
+
+    def reduce_small():
+        flip_x = (place.dp + 1 - 2 * (place.dp % 2), core)
+        flip_y = (place.dp + 2 - 4 * ((place.dp // 2) % 2), core)
+        current = small
+        for slot, device in enumerate((place.sibling(), flip_x, flip_y)):
+            copy = send_small(slot, current.at[...], small_from.at[slot], device)
+            copy.wait_recv()
+            small_sums[slot] = current[...] + small_from[slot]
+            current = small_sums.at[slot]
+            yield
+        copies = [
+            send_small(2 + dz, current.at[...], small_from.at[2 + dz], place.peer(dz, 0, 0))
+            for dz in range(1, 4)
+        ]
+        for copy in copies:
+            copy.wait_recv()
+        total = jnp.zeros(small.shape, jnp.float32)
+        small_from[2] = current[...]
+        for z in range(4):
+            total = total + small_from[2 + (place.z + 4 - z) % 4]
+        small_out[...] = total
+        yield
+
+    tiny = reduce_small()
+    flight = [to_sibling(which) for which in range(count)]
+    steps = (merge_cores, merge_b, merge_a, finish)
+    for turn in range(count + len(steps) - 1):
+        next(tiny, None)
+        for stage in range(len(steps)):
+            which = turn - stage
+            if 0 <= which < count:
+                flight[which] = steps[stage](which, flight[which])
+    for copy in flight:
+        copy.wait_recv()
+    for copy in started:
+        copy.wait_send()
+
+
+def reduce_blocks(grads, small):
+    count = len(grads)
+    dma = pltpu.SemaphoreType.DMA
+    blocks = [(g.shape[0] // 16, g.shape[1]) for g in grads]
+
+    def stages(*lead):
+        return [pltpu.VMEM((*lead, rows, columns // 2), jnp.bfloat16) for rows, columns in blocks]
+
+    scratch = [pltpu.VMEM((g.shape[0], g.shape[1] // 2), jnp.bfloat16) for g in grads]
+    scratch += stages(2, 2, 4) + stages(2, 4) + stages(4) + stages(3)
+    scratch += [
+        pltpu.VMEM((3, *small.shape), jnp.float32),
+        pltpu.VMEM((6, *small.shape), jnp.float32),
+        dma((count, 7)),
+        dma((count, 7)),
+        dma((6,)),
+        dma((6,)),
+    ]
+    return pl.pallas_call(
+        functools.partial(reduce_kernel, count),
+        out_shape=[jax.ShapeDtypeStruct(block, jnp.float32) for block in blocks]
+        + [jax.ShapeDtypeStruct(small.shape, jnp.float32)],
+        in_specs=[pl.BlockSpec(memory_space=pltpu.VMEM)] * (count + 1),
+        out_specs=[pl.BlockSpec(memory_space=pltpu.VMEM)] * (count + 1),
+        scratch_shapes=scratch,
+        compiler_params=pltpu.CompilerParams(
+            collective_id=1, has_side_effects=True, vmem_limit_bytes=58 * MIB
+        ),
+        name="reduce_grads",
+    )(*grads, small)
+
+
+GELU_A = 0.7978845608028654
+GELU_B = 0.044715
+
+
+def nt(left, right):
+    return lax.dot_general(left, right, (((1,), (1,)), ((), ())), preferred_element_type=jnp.float32)
+
+
+def tn(left, right):
+    return lax.dot_general(left, right, (((0,), (0,)), ((), ())), preferred_element_type=jnp.float32)
+
+
+def nn(left, right):
+    return jnp.dot(left, right, preferred_element_type=jnp.float32)
+
+
+def normalize(values):
+    center = jnp.mean(values, axis=-1, keepdims=True)
+    centered = values - center
+    spread = jnp.mean(centered * centered, axis=-1, keepdims=True)
+    scale = lax.rsqrt(spread + 1e-05)
+    return centered * scale, scale
+
+
+def normalize_back(grad, normed, scale, gain):
+    weighted = grad * gain
+    inner = weighted - jnp.mean(weighted, axis=-1, keepdims=True)
+    inner = inner - normed * jnp.mean(weighted * normed, axis=-1, keepdims=True)
+    return scale * inner
+
+
+def ffn_kernel(
+    tiles, lengths, normed, cotangent, resid, gain, up, down,
+    mixed, resid_grad, vectors, up_grad, down_grad,
+    grad_low, normed_t, out_sum, in_sum,
+):
+    step = pl.program_id(0)
+    slots, block_len = cotangent.shape[0], cotangent.shape[1]
+
+    @pl.when(step == 0)
+    def _():
+        base = lax.axis_index("seq") * block_len
+        spots = base + lax.broadcasted_iota(jnp.int32, (block_len, 1), 0)
+        for slot in range(slots):
+            keep = (spots < lengths[slot]).astype(jnp.float32)
+            grad_low[slot * block_len : (slot + 1) * block_len] = (
+                cotangent[slot].astype(jnp.float32) * keep
+            ).astype(jnp.bfloat16)
+        normed_t[...] = normed[...].T
+        out_sum[...] = resid[...]
+        in_sum[...] = jnp.zeros_like(in_sum)
+
+    pre = nn(normed[...], up[...])
+    wide = nt(grad_low[...], down[...])
+    square = pre * pre
+    ramp = jnp.tanh(pre * (GELU_A + (GELU_A * GELU_B) * square))
+    half = 0.5 + 0.5 * ramp
+    slope = half + (0.5 * pre) * (1.0 - ramp * ramp) * (GELU_A + (3.0 * GELU_A * GELU_B) * square)
+    act = (pre * half).astype(jnp.bfloat16)
+    back = (wide * slope).astype(jnp.bfloat16)
+    out_sum[...] += nn(act, down[...])
+    in_sum[...] += nt(back, up[...])
+    up_grad[...] = nn(normed_t[...], back).astype(jnp.bfloat16)
+    down_grad[...] = tn(act, grad_low[...]).astype(jnp.bfloat16)
+
+    @pl.when(step == tiles - 1)
+    def _():
+        gain_row = gain[...]
+        sums = jnp.zeros((2, resid.shape[1]), jnp.float32)
+        for slot in range(slots):
+            rows = slice(slot * block_len, (slot + 1) * block_len)
+            mixed[slot] = out_sum[rows].astype(jnp.bfloat16)
+            hat, scale = normalize(resid[rows])
+            grad = in_sum[rows]
+            sums = sums + jnp.concatenate(
+                [jnp.sum(grad * hat, axis=0, keepdims=True), jnp.sum(grad, axis=0, keepdims=True)],
+                axis=0,
+            )
+            resid_grad[rows] = grad_low[rows].astype(jnp.float32) + normalize_back(
+                grad, hat, scale, gain_row
+            )
+        vectors[...] = sums
+
+
+def feed_forward(normed, cotangent, resid, gain, up_full, down_full, lengths, tiles=6):
+    tokens, width = normed.shape
+    hidden = up_full.shape[1]
+    tile = hidden // tiles
+    whole = lambda *shape: pl.BlockSpec(shape, lambda i, *_: (0,) * len(shape))
+    return pl.pallas_call(
+        functools.partial(ffn_kernel, tiles),
+        grid_spec=pltpu.PrefetchScalarGridSpec(
+            num_scalar_prefetch=1,
+            grid=(tiles,),
+            in_specs=[
+                whole(tokens, width),
+                whole(*cotangent.shape),
+                whole(tokens, width),
+                whole(1, width),
+                pl.BlockSpec((width, tile), lambda i, *_: (0, i)),
+                pl.BlockSpec((tile, width), lambda i, *_: (i, 0)),
+            ],
+            out_specs=[
+                whole(*cotangent.shape),
+                whole(tokens, width),
+                whole(2, width),
+                pl.BlockSpec((width, tile), lambda i, *_: (0, i)),
+                pl.BlockSpec((tile, width), lambda i, *_: (i, 0)),
+            ],
+            scratch_shapes=[
+                pltpu.VMEM((tokens, width), jnp.bfloat16),
+                pltpu.VMEM((width, tokens), jnp.bfloat16),
+                pltpu.VMEM((tokens, width), jnp.float32),
+                pltpu.VMEM((tokens, width), jnp.float32),
+            ],
+        ),
+        out_shape=[
+            jax.ShapeDtypeStruct(cotangent.shape, jnp.bfloat16),
+            jax.ShapeDtypeStruct((tokens, width), jnp.float32),
+            jax.ShapeDtypeStruct((2, width), jnp.float32),
+            jax.ShapeDtypeStruct((width, hidden), jnp.bfloat16),
+            jax.ShapeDtypeStruct((hidden, width), jnp.bfloat16),
+        ],
+        compiler_params=pltpu.CompilerParams(vmem_limit_bytes=56 * MIB),
+        name="feed_forward",
+    )(lengths, normed, cotangent, resid, gain, up_full, down_full)
+
+
+PAIR = 2 * HEAD_DIM
+
+
+def lanes(pair):
+    return pl.ds(pl.multiple_of(pair * PAIR, PAIR), PAIR)
+
+
+def head_mask(rows, side):
+    spots = lax.broadcasted_iota(jnp.int32, (rows, PAIR), 1)
+    return (spots // HEAD_DIM) == side
+
+
+def only(mask, values):
+    return jnp.where(mask, values, jnp.zeros_like(values))
+
+
+def same_head():
+    first = lax.broadcasted_iota(jnp.int32, (PAIR, PAIR), 0) // HEAD_DIM
+    second = lax.broadcasted_iota(jnp.int32, (PAIR, PAIR), 1) // HEAD_DIM
+    return first == second
+
+
+def lower(size):
+    return lax.broadcasted_iota(jnp.int32, (size, size), 0) >= lax.broadcasted_iota(
+        jnp.int32, (size, size), 1
+    )
+
+
+def split(values):
+    high = values.astype(jnp.bfloat16)
+    low = (values - high.astype(jnp.float32)).astype(jnp.bfloat16)
+    return high, low
+
+
+def spots_of(block_len):
+    return lax.broadcasted_iota(jnp.int32, (block_len, 1), 0).astype(jnp.float32)
+
+
+def meet_sibling(place):
+    barrier = pltpu.get_barrier_semaphore()
+    pl.semaphore_signal(barrier, inc=1, device_id=place.sibling(), device_id_type=MESH)
+    pl.semaphore_wait(barrier, 1)
+
+
+def to_core(place, source, target, send_sem, recv_sem):
+    return pltpu.make_async_remote_copy(
+        src_ref=source,
+        dst_ref=target,
+        send_sem=send_sem,
+        recv_sem=recv_sem,
+        device_id=place.sibling(),
+        device_id_type=MESH,
+    )
+
+
+def shifted_keys(keys, slot, window, taps):
+    block_len = keys.shape[1] - 8
+    total = taps[0:1] * keys[slot, 8 : 8 + block_len, window]
+    for lag in range(1, 4):
+        total = total + taps[lag : lag + 1] * keys[slot, 8 - lag : 8 - lag + block_len, window]
+    return total
+
+
+ROW_RATE, ROW_TAPS = 2, 5
+
+
+def mixer_kernel(
+    tokens, vectors, qkv_weight, out_weight,
+    normed, queries, key_rows, values, edges, state_in, mixed, resid, normed_two,
+    keys, summed, state_out, send_sem, recv_sem,
+):
+    slots, block_len, width = tokens.shape
+    pairs = width // PAIR
+    size = block_len // 2
+    place = Place()
+    meet_sibling(place)
+    first = place.core == 0
+    gain, bias = vectors[0:1], vectors[1:2]
+
+    for slot in range(slots):
+        rows = slice(slot * block_len, (slot + 1) * block_len)
+        hat, _ = normalize(tokens[slot].astype(jnp.float32))
+        normed[rows] = (hat * gain + bias).astype(jnp.bfloat16)
+
+    def project(third, target):
+        for slot in range(slots):
+            rows = slice(slot * block_len, (slot + 1) * block_len)
+            target[slot] = nn(
+                normed[rows], qkv_weight[:, third * width : (third + 1) * width]
+            ).astype(jnp.bfloat16)
+
+    project(1, key_rows)
+    edge_copy = to_core(
+        place, key_rows.at[:, pl.ds(block_len - 16, 16)], edges, send_sem.at[0], recv_sem.at[0]
+    )
+
+    @pl.when(first)
+    def _():
+        edge_copy.start()
+
+    project(2, values)
+    project(0, queries)
+
+    @pl.when(first)
+    def _():
+        edge_copy.wait_send()
+        edges[...] = jnp.zeros_like(edges)
+
+    @pl.when(place.core == 1)
+    def _():
+        edge_copy.wait_recv()
+
+    for slot in range(slots):
+        keys[slot, 0:8] = edges[slot].astype(jnp.float32)[8:16]
+        keys[slot, 8:] = key_rows[slot].astype(jnp.float32)
+    spots = spots_of(block_len)
+    state_copy = to_core(place, state_out, state_in, send_sem.at[1], recv_sem.at[1])
+
+    @pl.when(first)
+    def _():
+        def fresh(pair, carry):
+            window = lanes(pair)
+            rate = vectors[ROW_RATE : ROW_RATE + 1, window]
+            taps = vectors[ROW_TAPS : ROW_TAPS + 4, window]
+            tail = jnp.exp(-rate * (block_len - 1.0 - spots))
+            for slot in range(slots):
+                tail_keys = (shifted_keys(keys, slot, window, taps) * tail).astype(jnp.bfloat16)
+                state_out[pair, slot] = only(same_head(), tn(tail_keys, values[slot, :, window]))
+            return carry
+
+        lax.fori_loop(0, pairs, fresh, 0)
+        state_copy.start()
+
+    def within(pair, carry):
+        window = lanes(pair)
+        rate = vectors[ROW_RATE : ROW_RATE + 1, window]
+        taps = vectors[ROW_TAPS : ROW_TAPS + 4, window]
+        fall = jnp.exp(-rate * spots)
+        rise = jnp.exp(rate * spots)
+        for slot in range(slots):
+            decayed = (queries[slot, :, window].astype(jnp.float32) * fall).astype(jnp.bfloat16)
+            lifted = (shifted_keys(keys, slot, window, taps) * rise).astype(jnp.bfloat16)
+            value = values[slot, :, window]
+            top = jnp.zeros((size, PAIR), jnp.float32)
+            low = jnp.zeros((size, PAIR), jnp.float32)
+            for side in range(2):
+                query_side = only(head_mask(block_len, side), decayed)
+                value_side = only(head_mask(block_len, side), value)
+                near = jnp.where(lower(size), nt(query_side[:size], lifted[:size]), 0.0)
+                top = top + nn(near.astype(jnp.bfloat16), value_side[:size])
+                far = nt(query_side[size:], lifted[:size]).astype(jnp.bfloat16)
+                near = jnp.where(lower(size), nt(query_side[size:], lifted[size:]), 0.0)
+                low = low + nn(far, value_side[:size]) + nn(near.astype(jnp.bfloat16), value_side[size:])
+            summed[slot, :size, window] = top
+            summed[slot, size:, window] = low
+        return carry
+
+    lax.fori_loop(0, pairs, within, 0)
+
+    @pl.when(first)
+    def _():
+        state_copy.wait_send()
+        state_in[...] = jnp.zeros_like(state_in)
+
+    @pl.when(place.core == 1)
+    def _():
+        state_copy.wait_recv()
+
+        def reach(pair, carry):
+            window = lanes(pair)
+            rate = vectors[ROW_RATE : ROW_RATE + 1, window]
+            decay = jnp.exp(-rate * (spots + 1.0))
+            for slot in range(slots):
+                reaching = (queries[slot, :, window].astype(jnp.float32) * decay).astype(jnp.bfloat16)
+                high, low = split(state_in[pair, slot])
+                summed[slot, :, window] += nn(reaching, high) + nn(reaching, low)
+            return carry
+
+        lax.fori_loop(0, pairs, reach, 0)
+
+    gain_two, bias_two = vectors[3:4], vectors[4:5]
+    for slot in range(slots):
+        rows = slice(slot * block_len, (slot + 1) * block_len)
+        mixed[rows] = summed[slot].astype(jnp.bfloat16)
+        total = tokens[slot].astype(jnp.float32) + nn(mixed[rows], out_weight[...])
+        resid[rows] = total
+        hat, _ = normalize(total)
+        normed_two[rows] = (hat * gain_two + bias_two).astype(jnp.bfloat16)
+
+
+def mixer_forward(tokens, vectors, qkv_weight, out_weight):
+    slots, block_len, width = tokens.shape
+    count = slots * block_len
+    pairs = width // PAIR
+    low, wide = jnp.bfloat16, jnp.float32
+    shape = jax.ShapeDtypeStruct
+    vmem = pl.BlockSpec(memory_space=pltpu.VMEM)
+    outs = [
+        shape((count, width), low),
+        shape((slots, block_len, width), low),
+        shape((slots, block_len, width), low),
+        shape((slots, block_len, width), low),
+        shape((slots, 16, width), low),
+        shape((pairs, slots, PAIR, PAIR), wide),
+        shape((count, width), low),
+        shape((count, width), wide),
+        shape((count, width), low),
+    ]
+    return pl.pallas_call(
+        mixer_kernel,
+        out_shape=outs,
+        in_specs=[vmem] * 4,
+        out_specs=[vmem] * len(outs),
+        scratch_shapes=[
+            pltpu.VMEM((slots, block_len + 8, width), wide),
+            pltpu.VMEM((slots, block_len, width), wide),
+            pltpu.VMEM((pairs, slots, PAIR, PAIR), wide),
+            pltpu.SemaphoreType.DMA((2,)),
+            pltpu.SemaphoreType.DMA((2,)),
+        ],
+        compiler_params=pltpu.CompilerParams(
+            collective_id=2, has_side_effects=True, vmem_limit_bytes=56 * MIB
+        ),
+        name="mixer_forward",
+    )(tokens, vectors, qkv_weight, out_weight)
+
+
+def mixer_back_kernel(
+    resid_grad, mixed, queries, key_rows, values, edges, state_in, normed, tokens, vectors,
+    qkv_weight, out_weight,
+    input_grad, out_grad, qkv_grad, small,
+    keys, branch, back_rows, projected, key_back, turned, state_send, state_grad, send_sem, recv_sem,
+):
+    slots, block_len, width = tokens.shape
+    pairs = width // PAIR
+    size = block_len // 2
+    low_type = jnp.bfloat16
+    place = Place()
+    meet_sibling(place)
+    first = place.core == 0
+    spots = spots_of(block_len)
+
+    for slot in range(slots):
+        rows = slice(slot * block_len, (slot + 1) * block_len)
+        branch[rows] = resid_grad[rows].astype(low_type)
+        back_rows[slot] = nt(branch[rows], out_weight[...]).astype(low_type)
+    state_copy = to_core(place, state_send, state_grad, send_sem.at[0], recv_sem.at[0])
+
+    @pl.when(place.core == 1)
+    def _():
+        def gather_state(pair, carry):
+            window = lanes(pair)
+            rate = vectors[ROW_RATE : ROW_RATE + 1, window]
+            decay = jnp.exp(-rate * (spots + 1.0))
+            for slot in range(slots):
+                reaching = (queries[slot, :, window].astype(jnp.float32) * decay).astype(low_type)
+                back = back_rows[slot, :, window]
+                state_send[pair, slot] = only(same_head(), tn(reaching, back)).astype(low_type)
+            return carry
+
+        lax.fori_loop(0, pairs, gather_state, 0)
+        state_copy.start()
+
+    turned[...] = mixed[...].T
+    out_grad[...] = nn(turned[...], branch[...]).astype(low_type)
+    for slot in range(slots):
+        keys[slot, 0:8] = edges[slot].astype(jnp.float32)[8:16]
+        keys[slot, 8:] = key_rows[slot].astype(jnp.float32)
+
+    @pl.when(place.core == 1)
+    def _():
+        state_copy.wait_send()
+        state_grad[...] = jnp.zeros_like(state_grad)
+
+    @pl.when(first)
+    def _():
+        state_copy.wait_recv()
+
+    def back_pair(pair, carry):
+        window = lanes(pair)
+        rate = vectors[ROW_RATE : ROW_RATE + 1, window]
+        taps = vectors[ROW_TAPS : ROW_TAPS + 4, window]
+        fall = jnp.exp(-rate * spots)
+        rise = jnp.exp(rate * spots)
+        tail = jnp.exp(-rate * (block_len - 1.0 - spots))
+        decay = jnp.exp(-rate * (spots + 1.0))
+        rate_grad = jnp.zeros((1, PAIR), jnp.float32)
+        taps_grad = [jnp.zeros((1, PAIR), jnp.float32) for _ in range(4)]
+        for slot in range(slots):
+            query = queries[slot, :, window].astype(jnp.float32)
+            key = shifted_keys(keys, slot, window, taps)
+            value = values[slot, :, window]
+            back = back_rows[slot, :, window]
+            wide_decayed, wide_lifted = query * fall, key * rise
+            wide_tail, wide_reach = key * tail, query * decay
+            decayed, lifted = wide_decayed.astype(low_type), wide_lifted.astype(low_type)
+            tail_keys = wide_tail.astype(low_type)
+            decayed_turned, back_turned = decayed.T, back.T
+            decayed_top = jnp.zeros((size, PAIR), jnp.float32)
+            decayed_low = jnp.zeros((size, PAIR), jnp.float32)
+            lifted_top = jnp.zeros((PAIR, size), jnp.float32)
+            lifted_low = jnp.zeros((PAIR, size), jnp.float32)
+            value_top = jnp.zeros((PAIR, size), jnp.float32)
+            value_low = jnp.zeros((PAIR, size), jnp.float32)
+            row_head = lax.broadcasted_iota(jnp.int32, (PAIR, block_len), 0) // HEAD_DIM
+            for side in range(2):
+                mask = head_mask(block_len, side)
+                query_side, back_side = only(mask, decayed), only(mask, back)
+                lifted_side = only(mask, lifted)
+                query_turned = only(row_head == side, decayed_turned)
+                back_side_turned = only(row_head == side, back_turned)
+                causal = lower(size)
+                halves = (slice(0, size), slice(size, block_len))
+                for t, s in ((0, 0), (1, 0), (1, 1)):
+                    score = nt(query_side[halves[t]], lifted[halves[s]])
+                    grad = nt(back_side[halves[t]], value[halves[s]])
+                    if t == s:
+                        score, grad = jnp.where(causal, score, 0.0), jnp.where(causal, grad, 0.0)
+                    score, grad = score.astype(low_type), grad.astype(low_type)
+                    query_part = nn(grad, lifted_side[halves[s]])
+                    lifted_part = nn(query_turned[:, halves[t]], grad)
+                    value_part = nn(back_side_turned[:, halves[t]], score)
+                    if t == 0:
+                        decayed_top = decayed_top + query_part
+                    else:
+                        decayed_low = decayed_low + query_part
+                    if s == 0:
+                        lifted_top, value_top = lifted_top + lifted_part, value_top + value_part
+                    else:
+                        lifted_low, value_low = lifted_low + lifted_part, value_low + value_part
+            decayed_grad = jnp.concatenate([decayed_top, decayed_low], axis=0)
+            lifted_grad = jnp.concatenate([lifted_top.T, lifted_low.T], axis=0)
+            value_grad = jnp.concatenate([value_top.T, value_low.T], axis=0)
+            leaving = state_grad[pair, slot]
+            entering = state_in[pair, slot]
+            high, low = split(entering)
+            value_grad = value_grad + nn(tail_keys, leaving)
+            tail_grad = nt(value, leaving)
+            reach_grad = nt(back, high) + nt(back, low)
+            carry_grad = jnp.sum((leaving.astype(jnp.float32) * entering).T, axis=0, keepdims=True)
+            key_grad = lifted_grad * rise + tail_grad * tail
+            steps = (
+                spots * (lifted_grad * wide_lifted - decayed_grad * wide_decayed)
+                - (block_len - 1.0 - spots) * (tail_grad * wide_tail)
+                - (spots + 1.0) * (reach_grad * wide_reach)
+            )
+            rate_grad = rate_grad + jnp.sum(steps, axis=0, keepdims=True)
+            rate_grad = rate_grad - block_len * jnp.exp(-rate * block_len) * carry_grad
+            projected[0, slot, :, window] = (decayed_grad * fall + reach_grad * decay).astype(low_type)
+            projected[2, slot, :, window] = value_grad.astype(low_type)
+            key_back[slot, 0:block_len, window] = key_grad
+            for lag in range(4):
+                lagged = keys[slot, 8 - lag : 8 - lag + block_len, window]
+                taps_grad[lag] = taps_grad[lag] + jnp.sum(lagged * key_grad, axis=0, keepdims=True)
+        small[0:8, window] = jnp.concatenate(
+            [jnp.zeros((2, PAIR), jnp.float32), rate_grad, *taps_grad, jnp.zeros((1, PAIR), jnp.float32)],
+            axis=0,
+        )
+        return carry
+
+    lax.fori_loop(0, pairs, back_pair, 0)
+    spill = to_core(
+        place,
+        key_back.at[:, pl.ds(0, 8)],
+        key_back.at[:, pl.ds(block_len, 8)],
+        send_sem.at[1],
+        recv_sem.at[1],
+    )
+
+    @pl.when(place.core == 1)
+    def _():
+        spill.start()
+        key_back[:, block_len : block_len + 8] = jnp.zeros((slots, 8, width), jnp.float32)
+
+    turned[...] = normed[...].T
+
+    def weight_grad(third):
+        for slot in range(1):
+            rows = projected[third].reshape(slots * block_len, width)
+            qkv_grad[:, third * width : (third + 1) * width] = nn(turned[...], rows).astype(low_type)
+
+    weight_grad(2)
+    weight_grad(0)
+
+    @pl.when(first)
+    def _():
+        spill.wait_recv()
+
+    def key_pair(pair, carry):
+        window = lanes(pair)
+        taps = vectors[ROW_TAPS : ROW_TAPS + 4, window]
+        for slot in range(slots):
+            total = taps[0:1] * key_back[slot, 0:block_len, window]
+            for lag in range(1, 4):
+                total = total + taps[lag : lag + 1] * key_back[slot, lag : lag + block_len, window]
+            projected[1, slot, :, window] = total.astype(low_type)
+        return carry
+
+    lax.fori_loop(0, pairs, key_pair, 0)
+    weight_grad(1)
+    gain = vectors[0:1]
+    sums = jnp.zeros((2, width), jnp.float32)
+    for slot in range(slots):
+        rows = slice(slot * block_len, (slot + 1) * block_len)
+        grad = nt(projected[0, slot], qkv_weight[:, 0:width])
+        for third in range(1, 3):
+            grad = grad + nt(projected[third, slot], qkv_weight[:, third * width : (third + 1) * width])
+        hat, scale = normalize(tokens[slot].astype(jnp.float32))
+        sums = sums + jnp.concatenate(
+            [jnp.sum(grad * hat, axis=0, keepdims=True), jnp.sum(grad, axis=0, keepdims=True)], axis=0
+        )
+        input_grad[slot] = resid_grad[rows] + normalize_back(grad, hat, scale, gain)
+    small[0:2] = sums
+
+    @pl.when(place.core == 1)
+    def _():
+        spill.wait_send()
+
+
+def mixer_backward(
+    resid_grad, mixed, queries, key_rows, values, edges, state_in, normed, tokens, vectors,
+    qkv_weight, out_weight,
+):
+    slots, block_len, width = tokens.shape
+    count = slots * block_len
+    pairs = width // PAIR
+    low, wide = jnp.bfloat16, jnp.float32
+    shape = jax.ShapeDtypeStruct
+    vmem = pl.BlockSpec(memory_space=pltpu.VMEM)
+    outs = [
+        shape(tokens.shape, wide),
+        shape((width, width), low),
+        shape((width, 3 * width), low),
+        shape((8, width), wide),
+    ]
+    return pl.pallas_call(
+        mixer_back_kernel,
+        out_shape=outs,
+        in_specs=[vmem] * 12,
+        out_specs=[vmem] * len(outs),
+        scratch_shapes=[
+            pltpu.VMEM((slots, block_len + 8, width), wide),
+            pltpu.VMEM((count, width), low),
+            pltpu.VMEM((slots, block_len, width), low),
+            pltpu.VMEM((3, slots, block_len, width), low),
+            pltpu.VMEM((slots, block_len + 8, width), wide),
+            pltpu.VMEM((width, count), low),
+            pltpu.VMEM((pairs, slots, PAIR, PAIR), low),
+            pltpu.VMEM((pairs, slots, PAIR, PAIR), low),
+            pltpu.SemaphoreType.DMA((2,)),
+            pltpu.SemaphoreType.DMA((2,)),
+        ],
+        compiler_params=pltpu.CompilerParams(
+            collective_id=3, has_side_effects=True, vmem_limit_bytes=58 * MIB
+        ),
+        name="mixer_backward",
+    )(
+        resid_grad, mixed, queries, key_rows, values, edges, state_in, normed, tokens, vectors,
+        qkv_weight, out_weight,
+    )
 
 
 def from_behind(value, axis, steps):
@@ -66,7 +1025,7 @@
     )
 
 
-def local(
+def general(
     tokens,
     ln1_gain,
     ln1_bias,
@@ -263,6 +1222,51 @@
     )
 
 
+def near(
+    tokens,
+    ln1_gain,
+    ln1_bias,
+    qkv_weight,
+    shift_taps,
+    decay_rates,
+    out_weight,
+    ln2_gain,
+    ln2_bias,
+    up_weight,
+    down_weight,
+    lengths,
+    out_grad,
+):
+    width = tokens.shape[2]
+    part = ln1_gain.shape[0]
+    packed = jnp.concatenate(
+        [jnp.stack([ln1_gain, ln1_bias, decay_rates, ln2_gain, ln2_bias]), shift_taps], axis=0
+    )
+    packed = jnp.pad(packed, ((0, 7), (0, 128 - part)))
+    qkv_full, out_full, up_full, down_full, wide = gather_blocks(
+        (qkv_weight, out_weight, up_weight, down_weight), packed
+    )
+    vectors = wide[:, :, :part].transpose(1, 0, 2).reshape(16, width).astype(jnp.float32)
+    normed, queries, key_rows, values, edges, state_in, mixer, resid, normed_two = mixer_forward(
+        tokens, vectors, qkv_full, out_full
+    )
+    mixed, resid_grad, two_sums, up_grad, down_grad = feed_forward(
+        normed_two, out_grad, resid, vectors[3:4], up_full, down_full, lengths
+    )
+    input_grad, proj_grad, qkv_grad, one_sums = mixer_backward(
+        resid_grad, mixer, queries, key_rows, values, edges, state_in, normed, tokens, vectors,
+        qkv_full, out_full,
+    )
+    small = jnp.concatenate([one_sums, two_sums, jnp.zeros((6, width), jnp.float32)], axis=0)
+    down_sum, up_sum, proj_sum, qkv_sum, small_sum = reduce_blocks(
+        (down_grad, up_grad, proj_grad, qkv_grad), small
+    )
+    own = lax.dynamic_slice(small_sum, (0, lax.axis_index("dp") * part), (16, part))
+    return (
+        mixed, input_grad, own[0], own[1], qkv_sum, own[3:7], own[2], proj_sum, own[8], own[9], up_sum, down_sum,
+    )
+
+
 def solution(mesh):
     in_specs = (
         P("dp", "seq", None),
@@ -293,4 +1297,5 @@
         P("dp", None),
         P("dp", None),
     )
+    local = near if dict(mesh.shape) == {"dp": 16, "seq": 2} else general
     return jax.shard_map(local, mesh=mesh, in_specs=in_specs, out_specs=out_specs, check_vma=False)

time: 1190 us -> 314 us (0.26)
  waiting for transfers between devices: 687 us -> 0 us
  Pallas kernels: 0 us -> 299 us
  blocking collectives: 193 us -> 0 us
  matrix products: 192 us -> 0 us
  local copies, waits for them, and re-layouts: 52.4 us -> 11.2 us
  other arithmetic: 38.3 us -> 2.28 us
  between operations: 16.9 us -> 0.73 us
    reduce_scatter x4 -> x0, waiting for transfers between devices: 538 us -> none  [the longest x1 177 us: local(): lax.psum_scatter(up_grad, 'dp', scatter_dimension=0, tiled=True)]
    pallas_call x0 -> x5, Pallas kernels: none -> 299 us  [the longest x1 112 us: reduce_blocks(): pl.pallas_call(functools.partial(reduce_kernel, count), out_shape=[jax.Sh...]
    dot_general x24 -> x0, matrix products: 192 us -> none  [the longest x4 38.6 us: back_product(): lax.dot_general(grad_rows, weight, (((1,), (1,)), ((), ())), preferred_el...]
    unnamed x2 -> x0, blocking collectives: 154 us -> none
    all_gather x4 -> x0, waiting for transfers between devices: 92.6 us -> none  [the longest x1 70.5 us: local(): lax.all_gather(down_weight, 'dp', axis=0, tiled=True)]
    unnamed x11 -> x0, waiting for transfers between devices: 38.3 us -> none
    all_gather x1 -> x0, blocking collectives: 35.5 us -> none  [local(): lax.all_gather(shift_taps, 'dp', axis=1, tiled=True)]
    unnamed x147 -> x17, local copies, waits for them, and re-layouts: 26.2 us -> 4.74 us
  transfers between devices with their start and end apart: 14 -> 0, of which waited for: 8 -> 0; matrix products, arithmetic and copies ran while one was open for 16% -> 0% of each run, Pallas kernels for 0% -> 0%
where the time goes in v1:
time: 314 us; the launch traced here: 313 us
  Pallas kernels  299 us (95%)
  local copies, waits for them, and re-layouts  11.2 us (4%)
    pallas_call x1, Pallas kernels, reduce_blocks(): pl.pallas_call(functools.partial(reduce_kernel, count), out_shape=[jax.Sh...  112 us
    pallas_call x1, Pallas kernels, gather_blocks(): pl.pallas_call(functools.partial(gather_kernel, count), out_shape=shapes,...  71.5 us
    pallas_call x1, Pallas kernels, mixer_backward(): pl.pallas_call(mixer_back_kernel, out_shape=outs, in_specs=[vmem] * 12, o...  47.7 us
    pallas_call x1, Pallas kernels, feed_forward(): pl.pallas_call(functools.partial(ffn_kernel, tiles), grid_spec=pltpu.Pref...  42.6 us
    pallas_call x1, Pallas kernels, mixer_forward(): pl.pallas_call(mixer_kernel, out_shape=outs, in_specs=[vmem] * 4, out_spe...  25.5 us

profile of v1, /device:TPU:0, one launch (start us, length us, event | category | flops | bytes accessed | tf_op | source)
XLA Modules:
  0.0 313.0 jit_solution(10358278436526435878)
XLA Ops:
  0.6 1.5 concatenate.6
  2.2 0.6 pad.4.refs_4_
  2.8 71.5 %gather_weights.1 = (bf16[768,2304]{1,0:T(8,128)(2,1)}, bf16[768,768]{1,0:T(8,128)(2,1)}, bf16[768,3072]{1,0:T(8,128)(2,1)}, bf16[3072,768]{1,0:T(8,128)(2,1)}, bf16[16,16,128]{2,1,0:T(8,128)(2,1)}) custom-call(bf16[48,2304]{1,0:T(8,128)(2,1)} %refs_0_.1, bf16[48,768]{1,0:T(8,128)(2,1)} %refs_1_.1, bf16[48,3072]{1,0:T(8,128)(2,1)} %refs_2_.1, ...), custom_call_target="tpu_custom_call" | custom-call | tf_op jit(solution)/shard_map/gather_weights/pallas_call | solution.py:185
  74.3 0.9 convert_bitcast_fusion
  75.2 0.7 convert_element_type.11.vectors
  75.9 25.5 %mixer_forward.1 = (bf16[1024,768]{1,0:T(8,128)(2,1)}, bf16[2,512,768]{2,1,0:T(8,128)(2,1)}, bf16[2,512,768]{2,1,0:T(8,128)(2,1)}, bf16[2,512,768]{2,1,0:T(8,128...) custom-call(bf16[2,512,768]{2,1,0:T(8,128)(2,1)} %tokens.3, ...), custom_call_target="tpu_custom_call" | custom-call | tf_op jit(solution)/shard_map/mixer_forward/pallas_call | solution.py:718
  101.4 0.7 slice.29.gain
  102.1 42.6 %feed_forward.1 = (bf16[2,512,768]{2,1,0:T(8,128)(2,1)}, f32[1024,768]{1,0:T(8,128)}, f32[2,768]{1,0:T(2,128)}, bf16[768,3072]{1,0:T(8,128)(2,1)}, bf16[3072,768]{1,0:T(8,128)(2,1)}) custom-call(s32[2]{0:T(128)} %lengths.1, bf16[1024,768]{1,0:T(8,128)(2,1)} %get-tuple-element.43.normed, bf16[2,512,768]{2,1,0:T(8,128)(2,1)} %cotangent.1, ...), custom_call_target="tpu_custom_call" | custom-call | tf_op jit(solution)/shard_map/feed_forward/pallas_call | solution.py:471
  144.7 47.7 %mixer_backward.1 = (f32[2,512,768]{2,1,0:T(8,128)}, bf16[768,768]{1,0:T(8,128)(2,1)}, bf16[768,2304]{1,0:T(8,128)(2,1)}, f32[8,768]{1,0:T(8,128)}) custom-call(f32[1024,768]{1,0:T(8,128)} %get-tuple-element.48.resid_grad, bf16[1024,768]{1,0:T(8,128)(2,1)} %get-tuple-element.49.mixed, bf16[2,512,768]{2,1,0:T(8,128)(2,1)} %get-tuple-element.50.queries, ...), custom_call_target="tpu_custom_call" | custom-call | tf_op jit(solution)/shard_map/mixer_backward/pallas_call | solution.py:945
  192.4 0.1 pad.7.clone
  192.5 0.0 copy-done.5
  192.5 1.4 maximum_maximum_fusion.refs_4_
  193.9 111.6 %reduce_grads.1 = (f32[192,768]{1,0:T(8,128)}, f32[48,3072]{1,0:T(8,128)}, f32[48,768]{1,0:T(8,128)}, f32[48,2304]{1,0:T(8,128)}, f32[16,768]{1,0:T(8,128)}) custom-call(bf16[3072,768]{1,0:T(8,128)(2,1)} %get-tuple-element.57.refs_0_, bf16[768,3072]{1,0:T(8,128)(2,1)} %get-tuple-element.58.refs_1_, bf16[768,768]{1,0:T(8,128)(2,1)} %get-tuple-element.59.refs_2_, ...), custom_call_target="tpu_custom_call" | custom-call | tf_op jit(solution)/shard_map/reduce_grads/pallas_call | solution.py:368
  305.5 1.4 dynamic-slice.2
  306.9 1.4 dynamic-slice_bitcast_fusion
  308.3 0.0 copy-done
  308.3 0.0 copy-start.4
  308.3 1.7 copy.31
  310.0 0.0 copy-done.3
  310.0 0.8 copy.32
  310.7 0.0 copy-done.4
  310.7 0.7 copy.33
  311.4 0.8 copy.34
  312.2 0.8 copy.35
  (10 shorter events, 0.1 us)
Async XLA Ops:
  144.7 47.8 %copy-start.5 = (f32[2,768]{1,0:T(2,128)S(1)}, f32[2,768]{1,0:T(2,128)}, u32[]{:S(2)}) copy-start(f32[2,768]{1,0:T(2,128)} %get-tuple-element.62) | copy-start | bytes 18436
  193.9 114.4 %copy-start = (f32[2,512,768]{2,1,0:T(8,128)S(1)}, f32[2,512,768]{2,1,0:T(8,128)}, u32[]{:S(2)}) copy-start(f32[2,512,768]{2,1,0:T(8,128)} %get-tuple-element.86) | copy-start | bytes 9437188
  308.3 1.7 copy-start.3
  308.3 2.4 copy-start.4
  310.0 1.4 copy-start.2
  310.0 2.2 copy-start.1

commit v2 on v0

--- a/solution.py
+++ b/solution.py
@@ -1,13 +1,1229 @@
+import functools
+
 import jax
 import jax.numpy as jnp
 from jax import lax
+from jax.experimental import pallas as pl
+from jax.experimental.pallas import tpu as pltpu
 from jax.sharding import PartitionSpec as P
 
 HEADS = 12
 HEAD_DIM = 64
+PAIR = 2 * HEAD_DIM
+MESH = pl.DeviceIdType.MESH
+MIB = 2**20
+GELU_A = 0.7978845608028654
+GELU_B = 0.044715
+ROW_RATE, ROW_TAPS = 2, 5
+LOW = jnp.bfloat16
+WIDE = jnp.float32
 
 
 precise = lax.Precision.HIGHEST
+
+
+class Place:
+    def __init__(self):
+        self.dp = lax.axis_index("dp")
+        self.core = lax.axis_index("seq")
+        self.z = self.dp // 4
+        self.stride_a = 2 - self.core
+        self.stride_b = 1 + self.core
+        self.a = (self.dp // self.stride_a) % 2
+        self.b = (self.dp // self.stride_b) % 2
+
+    def spot(self, da, db):
+        return (self.a + da) % 2 * self.stride_a + (self.b + db) % 2 * self.stride_b
+
+    def sibling_spot(self, da, db):
+        return (self.b + da) % 2 * self.stride_b + (self.a + db) % 2 * self.stride_a
+
+    def peer(self, dz, da, db):
+        return ((self.z + dz) % 4 * 4 + self.spot(da, db), self.core)
+
+    def sibling(self):
+        return (self.dp, 1 - self.core)
+
+
+PEERS = ((1, 0, 0), (2, 0, 0), (3, 0, 0), (0, 1, 0), (0, 0, 1))
+
+
+def enter(place):
+    barrier = pltpu.get_barrier_semaphore()
+    for step in PEERS:
+        pl.semaphore_signal(barrier, inc=1, device_id=place.peer(*step), device_id_type=MESH)
+    pl.semaphore_signal(barrier, inc=1, device_id=place.sibling(), device_id_type=MESH)
+    pl.semaphore_wait(barrier, len(PEERS) + 1)
+
+
+def remote(source, target, send_sem, recv_sem, device):
+    return pltpu.make_async_remote_copy(
+        src_ref=source,
+        dst_ref=target,
+        send_sem=send_sem,
+        recv_sem=recv_sem,
+        device_id=device,
+        device_id_type=MESH,
+    )
+
+
+def part(start, size, step):
+    return pl.ds(pl.multiple_of(start, step), size)
+
+
+class Unit:
+    def __init__(self, shard, buffer, rows, lead=None, start=0, width=None, shared=False):
+        self.shard, self.buffer, self.rows, self.lead = shard, buffer, rows, lead
+        self.start, self.width, self.shared = start, width, shared
+
+    def columns(self, side):
+        if self.shared:
+            return slice(None)
+        return part(self.start + side * (self.width // 2), self.width // 2, 128)
+
+    def own(self, side):
+        row, columns = self.shard[1], self.shard[2]
+        if self.shared:
+            return self.shard[0]
+        return self.shard[0].at[
+            pl.ds(row, self.rows), part(columns + side * (self.width // 2), self.width // 2, 128)
+        ]
+
+    def slab(self, spot, columns):
+        rows = part(spot * self.rows, self.rows, 16)
+        if self.lead is None:
+            return self.buffer.at[:, rows, columns]
+        return self.buffer.at[pl.ds(self.lead, 4), rows, columns]
+
+    def block(self, z, spot, columns):
+        rows = part(spot * self.rows, self.rows, 16)
+        return self.buffer.at[z if self.lead is None else self.lead + z, rows, columns]
+
+
+class Gather:
+    def __init__(self, place, units, send_sem, recv_sem, local_sem):
+        self.place, self.units = place, units
+        self.send_sem, self.recv_sem, self.local_sem = send_sem, recv_sem, local_sem
+        self.events = []
+        self.ready = {}
+        count = len(units)
+        for turn in range(count + 2):
+            if turn < count:
+                self.events.append(functools.partial(self.after_z, turn))
+            if 1 <= turn < count + 1:
+                self.events.append(functools.partial(self.after_a, turn - 1))
+            if 2 <= turn:
+                self.events.append(functools.partial(self.after_b, turn - 2))
+                self.ready[turn - 2] = len(self.events)
+        self.done = 0
+
+    def tick(self, count=1):
+        for event in self.events[self.done : self.done + count]:
+            event()
+        self.done = min(self.done + count, len(self.events))
+
+    def spread(self, index, trips, each):
+        for trip in range(trips):
+            chosen = self.events[self.done : self.done + each]
+            self.done += len(chosen)
+            if chosen:
+                @pl.when(index == trip)
+                def _(chosen=chosen):
+                    for event in chosen:
+                        event()
+
+    def need(self, which):
+        self.tick(max(0, self.ready[which] - self.done))
+        self.land(which)
+
+    def land(self, which):
+        unit = self.units[which]
+        if unit.shared:
+            return
+        other = unit.columns(1 - self.place.core)
+        for slot, (da, db) in enumerate(((0, 0), (1, 0), (0, 1), (1, 1))):
+            window = unit.slab(self.place.sibling_spot(da, db), other)
+            pltpu.make_async_copy(window, window, self.recv_sem.at[which, 6 + slot]).wait()
+
+    def copy(self, which, slot):
+        unit, place = self.units[which], self.place
+        mine = unit.columns(place.core)
+        if slot < 3:
+            step = (slot + 1, 0, 0)
+            source = unit.own(place.core)
+            target = unit.block(place.z, place.spot(0, 0), mine)
+            landing = 2 - slot
+            device = place.peer(*step)
+        else:
+            da, db = {3: (0, 0), 4: (0, 0), 5: (1, 0), 6: (0, 0), 7: (1, 0), 8: (0, 1), 9: (1, 1)}[slot]
+            source = target = unit.slab(place.spot(da, db), mine)
+            landing = slot
+            if slot == 3:
+                device = place.peer(0, 1, 0)
+            elif slot < 6:
+                device = place.peer(0, 0, 1)
+            else:
+                device = place.sibling()
+        return remote(
+            source, target, self.send_sem.at[which, slot], self.recv_sem.at[which, landing], device
+        )
+
+    def stay(self, which):
+        unit, place = self.units[which], self.place
+        return pltpu.make_async_copy(
+            unit.own(place.core),
+            unit.block(place.z, place.spot(0, 0), unit.columns(place.core)),
+            self.local_sem.at[which],
+        )
+
+    def start(self, which):
+        self.stay(which).start()
+        for slot in range(3):
+            self.copy(which, slot).start()
+
+    def arrive(self, which, slot):
+        unit, place = self.units[which], self.place
+        mine = unit.columns(place.core)
+        if slot < 3:
+            window = unit.block((place.z + slot + 1) % 4, place.spot(0, 0), mine)
+        else:
+            da, db = {3: (1, 0), 4: (0, 1), 5: (1, 1)}[slot]
+            window = unit.slab(place.spot(da, db), mine)
+        pltpu.make_async_copy(window, window, self.recv_sem.at[which, slot]).wait()
+
+    def pass_on(self, which, slot):
+        if not self.units[which].shared:
+            self.copy(which, slot).start()
+
+    def after_z(self, which):
+        self.stay(which).wait()
+        for slot in range(3):
+            self.arrive(which, slot)
+        self.copy(which, 3).start()
+        self.copy(which, 4).start()
+        self.pass_on(which, 6)
+
+    def after_a(self, which):
+        self.arrive(which, 3)
+        self.copy(which, 5).start()
+        self.pass_on(which, 7)
+
+    def after_b(self, which):
+        self.arrive(which, 4)
+        self.pass_on(which, 8)
+        self.arrive(which, 5)
+        self.pass_on(which, 9)
+
+    def drain(self):
+        for which, unit in enumerate(self.units):
+            for slot in range(6 if unit.shared else 10):
+                self.copy(which, slot).wait_send()
+
+
+def nt(left, right):
+    return lax.dot_general(left, right, (((1,), (1,)), ((), ())), preferred_element_type=WIDE)
+
+
+def tn(left, right):
+    return lax.dot_general(left, right, (((0,), (0,)), ((), ())), preferred_element_type=WIDE)
+
+
+def nn(left, right):
+    return jnp.dot(left, right, preferred_element_type=WIDE)
+
+
+def normalize(values):
+    center = jnp.mean(values, axis=-1, keepdims=True)
+    centered = values - center
+    spread = jnp.mean(centered * centered, axis=-1, keepdims=True)
+    scale = lax.rsqrt(spread + 1e-05)
+    return centered * scale, scale
+
+
+def normalize_back(grad, normed, scale, gain):
+    weighted = grad * gain
+    inner = weighted - jnp.mean(weighted, axis=-1, keepdims=True)
+    inner = inner - normed * jnp.mean(weighted * normed, axis=-1, keepdims=True)
+    return scale * inner
+
+
+def lanes(pair):
+    return pl.ds(pl.multiple_of(pair * PAIR, PAIR), PAIR)
+
+
+def head_mask(rows, side):
+    spots = lax.broadcasted_iota(jnp.int32, (rows, PAIR), 1)
+    return (spots // HEAD_DIM) == side
+
+
+def only(mask, values):
+    return jnp.where(mask, values, jnp.zeros_like(values))
+
+
+def same_head():
+    first = lax.broadcasted_iota(jnp.int32, (PAIR, PAIR), 0) // HEAD_DIM
+    second = lax.broadcasted_iota(jnp.int32, (PAIR, PAIR), 1) // HEAD_DIM
+    return first == second
+
+
+def lower(size):
+    return lax.broadcasted_iota(jnp.int32, (size, size), 0) >= lax.broadcasted_iota(
+        jnp.int32, (size, size), 1
+    )
+
+
+def split(values):
+    high = values.astype(LOW)
+    low = (values - high.astype(WIDE)).astype(LOW)
+    return high, low
+
+
+def spots_of(block_len):
+    return lax.broadcasted_iota(jnp.int32, (block_len, 1), 0).astype(WIDE)
+
+
+def shifted_keys(keys, slot, window, taps):
+    block_len = keys.shape[1] - 8
+    total = taps[0:1] * keys[slot, 8 : 8 + block_len, window]
+    for lag in range(1, 4):
+        total = total + taps[lag : lag + 1] * keys[slot, 8 - lag : 8 - lag + block_len, window]
+    return total
+
+
+def hidden_order(shard):
+    pieces = [
+        shard[:, device * 192 + lot * 64 : device * 192 + lot * 64 + 64]
+        for lot in range(3)
+        for device in range(16)
+    ]
+    return jnp.concatenate(pieces, axis=1)
+
+
+def hidden_disorder(columns):
+    pieces = [
+        columns[:, lot * 1024 + device * 64 : lot * 1024 + device * 64 + 64]
+        for device in range(16)
+        for lot in range(3)
+    ]
+    return jnp.concatenate(pieces, axis=1)
+
+
+VEC, KEY, VALUE, QUERY, OUT, DOWN, UP = range(7)
+
+
+def front_kernel(
+    lengths, packed, qkv_shard, out_shard, up_shard, down_shard, tokens_in, cotangent_in,
+    mixed_out, normed_out, qkv_out, edges_out, state_out, mixer_out, resid_grad_out, weights_out,
+    vectors_out, sums_out, up_out, down_out,
+    vec_all, weights, up_all, down_all, up_own, tokens, grad_low, normed, qkv, edges, state_in,
+    state_send, mixer, resid, normed_two, normed_turned, keys, summed, mixed, vectors, sums,
+    up_stage, down_stage, up_half, down_half,
+    send_sem, recv_sem, local_sem, load_sem, save_sem, pair_send, pair_recv, tile_send, tile_recv,
+):
+    slots, block_len, width = tokens.shape
+    pairs = width // PAIR
+    size = block_len // 2
+    tiles = up_half.shape[0]
+    place = Place()
+    core = place.core
+    first = core == 0
+    queries, key_rows, values = qkv.at[0], qkv.at[1], qkv.at[2]
+
+    def load(slot, source, target):
+        return pltpu.make_async_copy(source, target, load_sem.at[slot])
+
+    def save(slot):
+        source, target = (
+            (mixed, mixed_out), (normed, normed_out), (qkv, qkv_out), (edges, edges_out),
+            (state_in, state_out), (mixer, mixer_out), (keys.at[:, pl.ds(0, block_len)], resid_grad_out),
+            (weights, weights_out), (vectors, vectors_out), (sums, sums_out), (up_half, up_out),
+            (down_half, down_out),
+        )[slot]
+        return pltpu.make_async_copy(source, target, save_sem.at[slot])
+
+    load(0, up_shard, up_own).start()
+    load(1, tokens_in, tokens).start()
+    load(2, cotangent_in, grad_low).start()
+    enter(place)
+    units = [
+        Unit((packed, 0, 0), vec_all, 16, shared=True),
+        Unit((qkv_shard, 0, width), weights.at[1], 48, width=width),
+        Unit((qkv_shard, 0, 2 * width), weights.at[2], 48, width=width),
+        Unit((qkv_shard, 0, 0), weights.at[0], 48, width=width),
+        Unit((out_shard, 0, 0), weights.at[3], 48, width=width),
+    ]
+    for lot in range(3):
+        units.append(Unit((down_shard, lot * 64, 0), down_all, 64, lead=4 * lot, width=width))
+        units.append(Unit((up_own, 0, lot * 1024), up_all, 48, start=lot * 1024, width=1024))
+    gather = Gather(place, units, send_sem, recv_sem, local_sem)
+    for which in range(5):
+        gather.start(which)
+    load(0, up_shard, up_own).wait()
+    up_own[...] = hidden_order(up_own[...])
+    for which in range(5, len(units)):
+        gather.start(which)
+
+    load(1, tokens_in, tokens).wait()
+    gather.need(VEC)
+    vectors[...] = sum(
+        vec_all[z, spot * 16 : spot * 16 + 16].astype(WIDE) for z in range(4) for spot in range(4)
+    )
+    gain, bias = vectors[0:1], vectors[1:2]
+    for slot in range(slots):
+        rows = slice(slot * block_len, (slot + 1) * block_len)
+        hat, _ = normalize(tokens[slot].astype(WIDE))
+        normed[rows] = (hat * gain + bias).astype(LOW)
+    save(1).start()
+    save(8).start()
+    load(2, cotangent_in, grad_low).wait()
+    base = core * block_len
+    for slot in range(slots):
+        keep = base + lax.broadcasted_iota(jnp.int32, (block_len, 1), 0) < lengths[slot]
+        grad_low[slot] = (grad_low[slot].astype(WIDE) * keep.astype(WIDE)).astype(LOW)
+
+    def weight(which):
+        return weights[which].reshape(width, width)
+
+    def project(which):
+        for slot in range(slots):
+            rows = slice(slot * block_len, (slot + 1) * block_len)
+            qkv[which, slot] = nn(normed[rows], weight(which)).astype(LOW)
+
+    gather.need(KEY)
+    project(1)
+    edge_copy = remote(
+        key_rows.at[:, pl.ds(block_len - 16, 16)], edges, pair_send.at[0], pair_recv.at[0], place.sibling()
+    )
+
+    @pl.when(first)
+    def _():
+        edge_copy.start()
+
+    gather.need(VALUE)
+    project(2)
+    gather.need(QUERY)
+    project(0)
+    save(2).start()
+
+    @pl.when(first)
+    def _():
+        edge_copy.wait_send()
+        edges[...] = jnp.zeros_like(edges)
+
+    @pl.when(core == 1)
+    def _():
+        edge_copy.wait_recv()
+
+    save(3).start()
+    for slot in range(slots):
+        keys[slot, 0:8] = edges[slot].astype(WIDE)[8:16]
+        keys[slot, 8:] = key_rows[slot].astype(WIDE)
+    spots = spots_of(block_len)
+    state_copy = remote(state_send, state_in, pair_send.at[1], pair_recv.at[1], place.sibling())
+
+    @pl.when(first)
+    def _():
+        def fresh(pair, carry):
+            window = lanes(pair)
+            rate = vectors[ROW_RATE : ROW_RATE + 1, window]
+            taps = vectors[ROW_TAPS : ROW_TAPS + 4, window]
+            tail = jnp.exp(-rate * (block_len - 1.0 - spots))
+            for slot in range(slots):
+                tail_keys = (shifted_keys(keys, slot, window, taps) * tail).astype(LOW)
+                state_send[pair, slot] = only(same_head(), tn(tail_keys, values[slot, :, window]))
+            return carry
+
+        lax.fori_loop(0, pairs, fresh, 0)
+        state_copy.start()
+
+    gather.tick(2)
+
+    def within(pair, carry):
+        gather.spread(pair, pairs, TICKS_WITHIN)
+        window = lanes(pair)
+        rate = vectors[ROW_RATE : ROW_RATE + 1, window]
+        taps = vectors[ROW_TAPS : ROW_TAPS + 4, window]
+        fall = jnp.exp(-rate * spots)
+        rise = jnp.exp(rate * spots)
+        for slot in range(slots):
+            decayed = (queries[slot, :, window].astype(WIDE) * fall).astype(LOW)
+            lifted = (shifted_keys(keys, slot, window, taps) * rise).astype(LOW)
+            value = values[slot, :, window]
+            top = jnp.zeros((size, PAIR), WIDE)
+            low = jnp.zeros((size, PAIR), WIDE)
+            for side in range(2):
+                query_side = only(head_mask(block_len, side), decayed)
+                value_side = only(head_mask(block_len, side), value)
+                near = jnp.where(lower(size), nt(query_side[:size], lifted[:size]), 0.0)
+                top = top + nn(near.astype(LOW), value_side[:size])
+                far = nt(query_side[size:], lifted[:size]).astype(LOW)
+                near = jnp.where(lower(size), nt(query_side[size:], lifted[size:]), 0.0)
+                low = low + nn(far, value_side[:size]) + nn(near.astype(LOW), value_side[size:])
+            summed[slot, :size, window] = top
+            summed[slot, size:, window] = low
+        return carry
+
+    lax.fori_loop(0, pairs, within, 0)
+
+    @pl.when(first)
+    def _():
+        state_copy.wait_send()
+        state_in[...] = jnp.zeros_like(state_in)
+
+    @pl.when(core == 1)
+    def _():
+        state_copy.wait_recv()
+
+        def reach(pair, carry):
+            window = lanes(pair)
+            rate = vectors[ROW_RATE : ROW_RATE + 1, window]
+            decay = jnp.exp(-rate * (spots + 1.0))
+            for slot in range(slots):
+                reaching = (queries[slot, :, window].astype(WIDE) * decay).astype(LOW)
+                high, low = split(state_in[pair, slot])
+                summed[slot, :, window] += nn(reaching, high) + nn(reaching, low)
+            return carry
+
+        lax.fori_loop(0, pairs, reach, 0)
+
+    save(4).start()
+    gather.need(OUT)
+    save(7).start()
+    gain_two, bias_two = vectors[3:4], vectors[4:5]
+    for slot in range(slots):
+        rows = slice(slot * block_len, (slot + 1) * block_len)
+        mixer[rows] = summed[slot].astype(LOW)
+        total = tokens[slot].astype(WIDE) + nn(mixer[rows], weight(3))
+        resid[slot] = total
+        summed[slot] = total
+        hat, _ = normalize(total)
+        normed_two[rows] = (hat * gain_two + bias_two).astype(LOW)
+    save(5).start()
+    normed_turned[...] = normed_two[...].T
+    keys[:, 0:block_len] = jnp.zeros((slots, block_len, width), WIDE)
+    gather.need(DOWN)
+    gather.need(UP)
+
+    def tile_copies(tile):
+        slot = tile % 2
+        other = 1 - core
+        return (
+            remote(
+                up_stage.at[slot, :, part(other * 256, 256, 128)],
+                up_half.at[tile],
+                tile_send.at[tile, 0],
+                tile_recv.at[tile, 0],
+                place.sibling(),
+            ),
+            remote(
+                down_stage.at[slot, :, :, part(other * 384, 384, 128)],
+                down_half.at[pl.ds(2 * tile, 2)],
+                tile_send.at[tile, 1],
+                tile_recv.at[tile, 1],
+                place.sibling(),
+            ),
+        )
+
+    def merge(tile):
+        for copy in tile_copies(tile):
+            copy.wait_recv()
+        slot = tile % 2
+        up_half[tile] = up_half[tile] + up_stage[slot, :, part(core * 256, 256, 128)]
+        window = pl.ds(2 * tile, 2)
+        down_half[window] = down_half[window] + down_stage[slot, :, :, part(core * 384, 384, 128)]
+
+    def ffn_tile(tile, carry):
+        for lot in range(1, 3):
+            @pl.when(tile == 2 * lot)
+            def _(lot=lot):
+                gather.land(DOWN + 2 * lot)
+                gather.land(UP + 2 * lot)
+
+        columns = part(tile * 512, 512, 512)
+        up = up_all[:, :, columns].reshape(width, 512)
+        down = down_all[pl.ds(2 * tile, 2)].reshape(512, width)
+        cotangent = grad_low[...].reshape(slots * block_len, width)
+        pre = nn(normed_two[...], up)
+        wide = nt(cotangent, down)
+        square = pre * pre
+        ramp = jnp.tanh(pre * (GELU_A + (GELU_A * GELU_B) * square))
+        half = 0.5 + 0.5 * ramp
+        slope = half + (0.5 * pre) * (1.0 - ramp * ramp) * (
+            GELU_A + (3.0 * GELU_A * GELU_B) * square
+        )
+        act = (pre * half).astype(LOW)
+        back = (wide * slope).astype(LOW)
+        for slot in range(slots):
+            rows = slice(slot * block_len, (slot + 1) * block_len)
+            summed[slot] += nn(act[rows], down)
+            keys[slot, 0:block_len] += nt(back[rows], up)
+        turn = tile % 2
+
+        @pl.when(tile >= 2)
+        def _():
+            for copy in tile_copies(tile - 2):
+                copy.wait_send()
+
+        gather.spread(tile, tiles, TICKS_FFN)
+        up_stage[turn] = nn(normed_turned[...], back).astype(LOW)
+        down_stage[turn] = tn(act, cotangent).astype(LOW).reshape(2, 256, width)
+        for copy in tile_copies(tile):
+            copy.start()
+
+        @pl.when(tile >= 1)
+        def _():
+            merge(tile - 1)
+
+        return carry
+
+    lax.fori_loop(0, tiles, ffn_tile, 0)
+    sums[...] = jnp.zeros_like(sums)
+    for slot in range(slots):
+        mixed[slot] = summed[slot].astype(LOW)
+        hat, scale = normalize(resid[slot])
+        grad = keys[slot, 0:block_len]
+        sums[0:1] += jnp.sum(grad * hat, axis=0, keepdims=True)
+        sums[1:2] += jnp.sum(grad, axis=0, keepdims=True)
+        keys[slot, 0:block_len] = grad_low[slot].astype(WIDE) + normalize_back(grad, hat, scale, gain_two)
+    save(0).start()
+    save(6).start()
+    save(9).start()
+    merge(tiles - 1)
+    save(10).start()
+    save(11).start()
+    for tile in (tiles - 2, tiles - 1):
+        for copy in tile_copies(tile):
+            copy.wait_send()
+    gather.tick(len(gather.events))
+    gather.drain()
+    for slot in range(12):
+        save(slot).wait()
+
+
+TICKS_WITHIN, TICKS_FFN = 1, 3
+
+
+def front(packed, qkv_weight, out_weight, up_weight, down_weight, tokens, cotangent, lengths):
+    slots, block_len, width = tokens.shape
+    count = slots * block_len
+    pairs = width // PAIR
+    hidden = up_weight.shape[1]
+    tiles = hidden // 512
+    shape = jax.ShapeDtypeStruct
+    outs = [
+        shape(tokens.shape, LOW),
+        shape((count, width), LOW),
+        shape((3, slots, block_len, width), LOW),
+        shape((slots, 16, width), LOW),
+        shape((pairs, slots, PAIR, PAIR), WIDE),
+        shape((count, width), LOW),
+        shape(tokens.shape, WIDE),
+        shape((4, 4, width // 4, width), LOW),
+        shape((16, width), WIDE),
+        shape((8, width), WIDE),
+        shape((tiles, width, 256), LOW),
+        shape((2 * tiles, 256, width // 2), LOW),
+    ]
+    vmem = lambda *dims: pltpu.VMEM(dims, LOW)
+    wide = lambda *dims: pltpu.VMEM(dims, WIDE)
+    dma = pltpu.SemaphoreType.DMA
+    anywhere = pl.BlockSpec(memory_space=pltpu.HBM)
+    return pl.pallas_call(
+        front_kernel,
+        out_shape=outs,
+        in_specs=[pl.BlockSpec(memory_space=pltpu.SMEM)] + [anywhere] * 7,
+        out_specs=[anywhere] * len(outs),
+        scratch_shapes=[
+            vmem(4, 64, width),
+            vmem(4, 4, width // 4, width),
+            vmem(4, width // 4, hidden),
+            vmem(12, 256, width),
+            vmem(width // 16, hidden),
+            vmem(slots, block_len, width),
+            vmem(slots, block_len, width),
+            vmem(count, width),
+            vmem(3, slots, block_len, width),
+            vmem(slots, 16, width),
+            wide(pairs, slots, PAIR, PAIR),
+            wide(pairs, slots, PAIR, PAIR),
+            vmem(count, width),
+            wide(slots, block_len, width),
+            vmem(count, width),
+            vmem(width, count),
+            wide(slots, block_len + 8, width),
+            wide(slots, block_len, width),
+            vmem(slots, block_len, width),
+            wide(16, width),
+            wide(8, width),
+            vmem(2, width, 512),
+            vmem(2, 2, 256, width),
+            vmem(tiles, width, 256),
+            vmem(2 * tiles, 256, width // 2),
+            dma((11, 10)),
+            dma((11, 10)),
+            dma((11,)),
+            dma((3,)),
+            dma((12,)),
+            dma((2,)),
+            dma((2,)),
+            dma((tiles, 2)),
+            dma((tiles, 2)),
+        ],
+        compiler_params=pltpu.CompilerParams(
+            collective_id=0, has_side_effects=True, vmem_limit_bytes=63 * MIB
+        ),
+        name="gather_forward_ffn",
+    )(lengths, packed, qkv_weight, out_weight, up_weight, down_weight, tokens, cotangent)
+
+
+class Share:
+    def __init__(self, source, own, from_b, from_a, from_z, final, rows):
+        self.source, self.own, self.rows = source, own, rows
+        self.from_b, self.from_a, self.from_z, self.final = from_b, from_a, from_z, final
+
+    def slab(self, ref, spot):
+        return ref.at[:, part(spot * self.rows, self.rows, 16)]
+
+
+class Reduction:
+    def __init__(self, place, shares, send_sem, recv_sem):
+        self.place, self.shares = place, shares
+        self.send_sem, self.recv_sem = send_sem, recv_sem
+
+    def copy(self, which, slot):
+        share, place = self.shares[which], self.place
+        if slot < 2:
+            da = 1 - slot
+            source = share.slab(share.source, place.spot(da, 1))
+            target = share.from_b.at[(place.a + da) % 2]
+            device = place.peer(0, 0, 1)
+        elif slot == 2:
+            source, target = share.from_b.at[1 - place.a], share.from_a
+            device = place.peer(0, 1, 0)
+        elif slot < 6:
+            dz = slot - 2
+            source, target = share.from_a.at[(place.z + dz) % 4], share.from_z.at[dz - 1]
+            device = place.peer(dz, 0, 0)
+        else:
+            source = target = share.final.at[place.core]
+            device = place.sibling()
+        return remote(source, target, self.send_sem.at[which, slot], self.recv_sem.at[which, slot], device)
+
+    def start(self, which):
+        for slot in range(2):
+            self.copy(which, slot).start()
+
+    def merge_b(self, which):
+        share, place = self.shares[which], self.place
+        for slot in range(2):
+            self.copy(which, slot).wait_recv()
+            da = 1 - slot
+            a = (place.a + da) % 2
+            rows = part(place.spot(da, 0) * share.rows, share.rows, 16)
+            share.from_b[a] = share.from_b[a] + share.own[:, rows]
+            if slot == 0:
+                self.copy(which, 2).start()
+
+    def merge_a(self, which):
+        share = self.shares[which]
+        self.copy(which, 2).wait_recv()
+        share.from_a[...] = share.from_a[...] + share.from_b[self.place.a]
+        for slot in range(3, 6):
+            self.copy(which, slot).start()
+
+    def finish(self, which):
+        share, place = self.shares[which], self.place
+        total = share.from_a[place.z].astype(WIDE)
+        for slot in range(3):
+            self.copy(which, 3 + slot).wait_recv()
+            total = total + share.from_z[slot].astype(WIDE)
+        share.final[place.core] = total
+        self.copy(which, 6).start()
+
+    def land(self, which):
+        share, place = self.shares[which], self.place
+        other = share.final.at[1 - place.core]
+        pltpu.make_async_copy(other, other, self.recv_sem.at[which, 6]).wait()
+
+    def drain(self):
+        for which in range(len(self.shares)):
+            for slot in range(7):
+                self.copy(which, slot).wait_send()
+
+
+class Script:
+    def __init__(self, events):
+        self.events, self.done = events, 0
+
+    def tick(self, count):
+        for event in self.events[self.done : self.done + count]:
+            event()
+        self.done = min(self.done + count, len(self.events))
+
+    def spread(self, index, trips, each):
+        for trip in range(trips):
+            chosen = self.events[self.done : self.done + each]
+            self.done += len(chosen)
+            if chosen:
+                @pl.when(index == trip)
+                def _(chosen=chosen):
+                    for event in chosen:
+                        event()
+
+
+def staggered(reduction, which):
+    events = []
+    which = list(which)
+    for turn in range(len(which) + 2):
+        for lag, step in enumerate((reduction.merge_b, reduction.merge_a, reduction.finish)):
+            if 0 <= turn - lag < len(which):
+                events.append(functools.partial(step, which[turn - lag]))
+    return events
+
+
+UPS, DOWNS, OUTS, PAIRS, KEYS = 0, 6, 9, 10, 16
+
+
+def back_kernel(
+    resid_grad_in, mixer_in, qkv_in, edges_in, state_in_in, normed_in, tokens_in, weights_in,
+    vectors_in, two_sums, up_in, down_in,
+    input_grad_out, up_sum, down_sum, out_sum, qkv_sum, small_out,
+    resid_grad, mixer, qkv, edges, state_in, normed, weights, vectors, up_half, down_half,
+    keys, branch, back_rows, projected, key_back, normed_turned, state_send, state_grad,
+    out_stage, out_half, pair_stage, pair_half, key_half,
+    up_b, up_a, up_z, up_final, down_b, down_a, down_z, down_final, wide_b, wide_a, wide_z, wide_final,
+    pair_b, pair_a, pair_z, pair_final, small, small_sums, small_from,
+    send_sem, recv_sem, load_sem, save_sem, core_send, core_recv, pair_send, pair_recv,
+    small_send, small_recv,
+):
+    slots, block_len, width = resid_grad.shape
+    pairs = width // PAIR
+    size = block_len // 2
+    place = Place()
+    core = place.core
+    first = core == 0
+    second = core == 1
+    queries, key_rows, values = qkv.at[0], qkv.at[1], qkv.at[2]
+    inputs = (
+        (resid_grad_in, resid_grad), (weights_in, weights), (vectors_in, vectors), (qkv_in, qkv),
+        (mixer_in, mixer), (edges_in, edges), (state_in_in, state_in), (normed_in, normed),
+        (up_in, up_half), (down_in, down_half), (tokens_in, mixer),
+    )
+    LOAD_GRAD, LOAD_WEIGHTS, LOAD_VECTORS, LOAD_QKV, LOAD_MIXER, LOAD_EDGES, LOAD_STATE = range(7)
+    LOAD_NORMED, LOAD_UP, LOAD_DOWN, LOAD_TOKENS = range(7, 11)
+
+    def load(slot):
+        return pltpu.make_async_copy(*inputs[slot], load_sem.at[slot])
+
+    for slot in range(LOAD_TOKENS):
+        load(slot).start()
+    enter(place)
+    shares = [
+        Share(
+            up_in.at[k], up_half.at[k],
+            up_b.at[k], up_a.at[k], up_z.at[k], up_final.at[k], 48,
+        )
+        for k in range(6)
+    ]
+    shares += [
+        Share(
+            down_in.at[pl.ds(4 * k, 4)], down_half.at[pl.ds(4 * k, 4)],
+            down_b.at[k], down_a.at[k], down_z.at[k], down_final.at[k], 64,
+        )
+        for k in range(3)
+    ]
+    shares.append(
+        Share(out_half, out_half, wide_b.at[0], wide_a.at[0], wide_z.at[0], wide_final.at[0], 48)
+    )
+    shares += [
+        Share(
+            pair_half.at[k], pair_half.at[k], pair_b.at[k], pair_a.at[k], pair_z.at[k],
+            pair_final.at[k], 48,
+        )
+        for k in range(6)
+    ]
+    shares.append(
+        Share(key_half, key_half, wide_b.at[1], wide_a.at[1], wide_z.at[1], wide_final.at[1], 48)
+    )
+    reduction = Reduction(place, shares, send_sem, recv_sem)
+    for k in range(3):
+        reduction.start(UPS + 2 * k)
+        reduction.start(UPS + 2 * k + 1)
+        reduction.start(DOWNS + k)
+    script = Script(staggered(reduction, (0, 1, 6, 2, 3, 7, 4, 5, 8, 9)))
+    spots = spots_of(block_len)
+
+    load(LOAD_GRAD).wait()
+    load(LOAD_WEIGHTS).wait()
+    out_weight = weights[3].reshape(width, width)
+    for slot in range(slots):
+        rows = slice(slot * block_len, (slot + 1) * block_len)
+        branch[rows] = resid_grad[slot].astype(LOW)
+        back_rows[slot] = nt(branch[rows], out_weight).astype(LOW)
+    load(LOAD_VECTORS).wait()
+    load(LOAD_QKV).wait()
+    state_copy = remote(state_send, state_grad, core_send.at[0], core_recv.at[0], place.sibling())
+
+    @pl.when(second)
+    def _():
+        def gather_state(pair, carry):
+            window = lanes(pair)
+            rate = vectors[ROW_RATE : ROW_RATE + 1, window]
+            decay = jnp.exp(-rate * (spots + 1.0))
+            for slot in range(slots):
+                reaching = (queries[slot, :, window].astype(WIDE) * decay).astype(LOW)
+                back = back_rows[slot, :, window]
+                state_send[pair, slot] = only(same_head(), tn(reaching, back)).astype(LOW)
+            return carry
+
+        lax.fori_loop(0, pairs, gather_state, 0)
+        state_copy.start()
+
+    load(LOAD_MIXER).wait()
+    load(LOAD_UP).wait()
+    load(LOAD_DOWN).wait()
+    normed_turned[...] = mixer[...].T
+    out_stage[...] = nn(normed_turned[...], branch[...]).astype(LOW).reshape(4, width // 4, width)
+
+    def halves(stage, half, sem):
+        window = part((1 - core) * (width // 2), width // 2, 128)
+        return remote(stage.at[:, :, window], half, core_send.at[sem], core_recv.at[sem], place.sibling())
+
+    def own_half(stage, half):
+        half[...] = half[...] + stage[:, :, part(core * (width // 2), width // 2, 128)]
+
+    load(LOAD_TOKENS).start()
+    out_copy = halves(out_stage, out_half, 2)
+    out_copy.start()
+    load(LOAD_EDGES).wait()
+    load(LOAD_STATE).wait()
+    load(LOAD_NORMED).wait()
+    normed_turned[...] = normed[...].T
+    for slot in range(slots):
+        keys[slot, 0:8] = edges[slot].astype(WIDE)[8:16]
+        keys[slot, 8:] = key_rows[slot].astype(WIDE)
+    out_copy.wait_recv()
+    own_half(out_stage, out_half)
+    reduction.start(OUTS)
+
+    @pl.when(second)
+    def _():
+        state_copy.wait_send()
+        state_grad[...] = jnp.zeros_like(state_grad)
+
+    @pl.when(first)
+    def _():
+        state_copy.wait_recv()
+
+    def pair_copy(pair):
+        return remote(
+            pair_stage.at[pair, 1 - core], pair_half.at[pair], pair_send.at[pair], pair_recv.at[pair],
+            place.sibling(),
+        )
+
+    def merge_pair(pair):
+        pair_copy(pair).wait_recv()
+        pair_half[pair] = pair_half[pair] + pair_stage[pair, core]
+
+    def back_pair(pair, carry):
+        script.spread(pair, pairs, TICKS_BACK)
+        window = lanes(pair)
+        rate = vectors[ROW_RATE : ROW_RATE + 1, window]
+        taps = vectors[ROW_TAPS : ROW_TAPS + 4, window]
+        fall = jnp.exp(-rate * spots)
+        rise = jnp.exp(rate * spots)
+        tail = jnp.exp(-rate * (block_len - 1.0 - spots))
+        decay = jnp.exp(-rate * (spots + 1.0))
+        rate_grad = jnp.zeros((1, PAIR), WIDE)
+        taps_grad = [jnp.zeros((1, PAIR), WIDE) for _ in range(4)]
+        weight_grad = jnp.zeros((width, 2 * PAIR), WIDE)
+        for slot in range(slots):
+            query = queries[slot, :, window].astype(WIDE)
+            key = shifted_keys(keys, slot, window, taps)
+            value = values[slot, :, window]
+            back = back_rows[slot, :, window]
+            wide_decayed, wide_lifted = query * fall, key * rise
+            wide_tail, wide_reach = key * tail, query * decay
+            decayed, lifted = wide_decayed.astype(LOW), wide_lifted.astype(LOW)
+            tail_keys = wide_tail.astype(LOW)
+            decayed_turned, back_turned = decayed.T, back.T
+            decayed_top = jnp.zeros((size, PAIR), WIDE)
+            decayed_low = jnp.zeros((size, PAIR), WIDE)
+            lifted_top = jnp.zeros((PAIR, size), WIDE)
+            lifted_low = jnp.zeros((PAIR, size), WIDE)
+            value_top = jnp.zeros((PAIR, size), WIDE)
+            value_low = jnp.zeros((PAIR, size), WIDE)
+            row_head = lax.broadcasted_iota(jnp.int32, (PAIR, block_len), 0) // HEAD_DIM
+            for side in range(2):
+                mask = head_mask(block_len, side)
+                query_side, back_side = only(mask, decayed), only(mask, back)
+                lifted_side = only(mask, lifted)
+                query_turned = only(row_head == side, decayed_turned)
+                back_side_turned = only(row_head == side, back_turned)
+                causal = lower(size)
+                halves_of = (slice(0, size), slice(size, block_len))
+                for t, s in ((0, 0), (1, 0), (1, 1)):
+                    score = nt(query_side[halves_of[t]], lifted[halves_of[s]])
+                    grad = nt(back_side[halves_of[t]], value[halves_of[s]])
+                    if t == s:
+                        score, grad = jnp.where(causal, score, 0.0), jnp.where(causal, grad, 0.0)
+                    score, grad = score.astype(LOW), grad.astype(LOW)
+                    query_part = nn(grad, lifted_side[halves_of[s]])
+                    lifted_part = nn(query_turned[:, halves_of[t]], grad)
+                    value_part = nn(back_side_turned[:, halves_of[t]], score)
+                    if t == 0:
+                        decayed_top = decayed_top + query_part
+                    else:
+                        decayed_low = decayed_low + query_part
+                    if s == 0:
+                        lifted_top, value_top = lifted_top + lifted_part, value_top + value_part
+                    else:
+                        lifted_low, value_low = lifted_low + lifted_part, value_low + value_part
+            decayed_grad = jnp.concatenate([decayed_top, decayed_low], axis=0)
+            lifted_grad = jnp.concatenate([lifted_top.T, lifted_low.T], axis=0)
+            value_grad = jnp.concatenate([value_top.T, value_low.T], axis=0)
+            leaving = state_grad[pair, slot]
+            entering = state_in[pair, slot]
+            high, low = split(entering)
+            value_grad = value_grad + nn(tail_keys, leaving)
+            tail_grad = nt(value, leaving)
+            reach_grad = nt(back, high) + nt(back, low)
+            carry_grad = jnp.sum((leaving.astype(WIDE) * entering).T, axis=0, keepdims=True)
+            key_grad = lifted_grad * rise + tail_grad * tail
+            steps = (
+                spots * (lifted_grad * wide_lifted - decayed_grad * wide_decayed)
+                - (block_len - 1.0 - spots) * (tail_grad * wide_tail)
+                - (spots + 1.0) * (reach_grad * wide_reach)
+            )
+            rate_grad = rate_grad + jnp.sum(steps, axis=0, keepdims=True)
+            rate_grad = rate_grad - block_len * jnp.exp(-rate * block_len) * carry_grad
+            query_low = (decayed_grad * fall + reach_grad * decay).astype(LOW)
+            value_low_grad = value_grad.astype(LOW)
+            projected[0, slot, :, window] = query_low
+            projected[2, slot, :, window] = value_low_grad
+            key_back[slot, 0:block_len, window] = key_grad
+            for lag in range(4):
+                lagged = keys[slot, 8 - lag : 8 - lag + block_len, window]
+                taps_grad[lag] = taps_grad[lag] + jnp.sum(lagged * key_grad, axis=0, keepdims=True)
+            rows = slice(slot * block_len, (slot + 1) * block_len)
+            weight_grad = weight_grad + nn(
+                normed_turned[:, rows], jnp.concatenate([query_low, value_low_grad], axis=1)
+            )
+        small[0:8, window] = jnp.concatenate(
+            [jnp.zeros((2, PAIR), WIDE), rate_grad, *taps_grad, jnp.zeros((1, PAIR), WIDE)], axis=0
+        )
+        for side in range(2):
+            pair_stage[pair, side] = (
+                weight_grad[:, side * PAIR : (side + 1) * PAIR].astype(LOW).reshape(4, width // 4, PAIR)
+            )
+        pair_copy(pair).start()
+
+        @pl.when(pair >= 1)
+        def _():
+            merge_pair(pair - 1)
+
+        for k in range(1, pairs):
+            @pl.when(pair == k)
+            def _(k=k):
+                reduction.start(PAIRS + k - 1)
+
+        return carry
+
+    lax.fori_loop(0, pairs, back_pair, 0)
+    spill = remote(
+        key_back.at[:, pl.ds(0, 8)],
+        key_back.at[:, pl.ds(block_len, 8)],
+        core_send.at[1],
+        core_recv.at[1],
+        place.sibling(),
+    )
+
+    @pl.when(second)
+    def _():
+        spill.start()
+        key_back[:, block_len : block_len + 8] = jnp.zeros((slots, 8, width), WIDE)
+
+    script.tick(3)
+    merge_pair(pairs - 1)
+    reduction.start(PAIRS + pairs - 1)
+
+    @pl.when(first)
+    def _():
+        spill.wait_recv()
+
+    def key_pair(pair, carry):
+        window = lanes(pair)
+        taps = vectors[ROW_TAPS : ROW_TAPS + 4, window]
+        for slot in range(slots):
+            total = taps[0:1] * key_back[slot, 0:block_len, window]
+            for lag in range(1, 4):
+                total = total + taps[lag : lag + 1] * key_back[slot, lag : lag + block_len, window]
+            projected[1, slot, :, window] = total.astype(LOW)
+        return carry
+
+    lax.fori_loop(0, pairs, key_pair, 0)
+    rows_all = projected[1].reshape(slots * block_len, width)
+    out_copy.wait_send()
+    out_stage[...] = nn(normed_turned[...], rows_all).astype(LOW).reshape(4, width // 4, width)
+    key_copy = halves(out_stage, key_half, 3)
+    key_copy.start()
+    script.tick(len(script.events))
+    late = Script(staggered(reduction, (*range(PAIRS, PAIRS + pairs), KEYS)))
+    late.tick(3)
+    load(LOAD_TOKENS).wait()
+    gain = vectors[0:1]
+    key_copy.wait_recv()
+    own_half(out_stage, key_half)
+    reduction.start(KEYS)
+    gain_sum = jnp.zeros((1, width), WIDE)
+    bias_sum = jnp.zeros((1, width), WIDE)
+    for slot in range(slots):
+        late.tick(4)
+        grad = nt(projected[0, slot], weights[0].reshape(width, width))
+        for third in range(1, 3):
+            grad = grad + nt(projected[third, slot], weights[third].reshape(width, width))
+        hat, scale = normalize(mixer[slot * block_len : (slot + 1) * block_len].astype(WIDE))
+        gain_sum = gain_sum + jnp.sum(grad * hat, axis=0, keepdims=True)
+        bias_sum = bias_sum + jnp.sum(grad, axis=0, keepdims=True)
+        resid_grad[slot] = resid_grad[slot] + normalize_back(grad, hat, scale, gain)
+        pltpu.make_async_copy(
+            resid_grad.at[slot], input_grad_out.at[slot], save_sem.at[slot]
+        ).start()
+    small[0:1], small[1:2] = gain_sum, bias_sum
+    small[8:16] = two_sums[...]
+
+    def small_copy(slot):
+        flip_x = (place.dp + 1 - 2 * (place.dp % 2), core)
+        flip_y = (place.dp + 2 - 4 * ((place.dp // 2) % 2), core)
+        source = small if slot == 0 else small_sums.at[min(slot, 3) - 1]
+        device = (place.sibling(), flip_x, flip_y)[slot] if slot < 3 else place.peer(slot - 2, 0, 0)
+        return remote(source, small_from.at[slot], small_send.at[slot], small_recv.at[slot], device)
+
+    small_copy(0).start()
+    for slot in range(3):
+        late.tick(2)
+        small_copy(slot).wait_recv()
+        before = small[...] if slot == 0 else small_sums[slot - 1]
+        small_sums[slot] = before + small_from[slot]
+        if slot < 2:
+            small_copy(slot + 1).start()
+    for slot in range(3, 6):
+        small_copy(slot).start()
+    late.tick(len(late.events))
+    for slot in range(3, 6):
+        small_copy(slot).wait_recv()
+    small_from[2] = small_sums[2]
+    total = jnp.zeros(small.shape, WIDE)
+    for z in range(4):
+        total = total + small_from[2 + (place.z + 4 - z) % 4]
+    small_out[...] = total
+    for which in range(len(shares)):
+        reduction.land(which)
+    ups = [up_final[tile, side] for tile in range(6) for side in range(2)]
+    up_sum[...] = hidden_disorder(jnp.concatenate(ups, axis=1))
+    for lot in range(3):
+        for side in range(2):
+            down_sum[lot * 64 : lot * 64 + 64, side * 384 : side * 384 + 384] = down_final[lot, side]
+    for side in range(2):
+        out_sum[:, side * 384 : side * 384 + 384] = wide_final[0, side]
+        qkv_sum[:, width + side * 384 : width + side * 384 + 384] = wide_final[1, side]
+        for pair in range(pairs):
+            start = 2 * width * side + pair * PAIR
+            qkv_sum[:, start : start + PAIR] = pair_final[pair, side]
+    reduction.drain()
+    for slot in range(6):
+        small_copy(slot).wait_send()
+    for pair in range(pairs):
+        pair_copy(pair).wait_send()
+    key_copy.wait_send()
+
+    @pl.when(second)
+    def _():
+        spill.wait_send()
+
+    for slot in range(slots):
+        pltpu.make_async_copy(
+            resid_grad.at[slot], input_grad_out.at[slot], save_sem.at[slot]
+        ).wait()
+
+
+TICKS_BACK = 4
+
+
+def back(
+    resid_grad, mixer, qkv, edges, state_in, normed, tokens, weights, vectors, two_sums, up_half, down_half,
+):
+    slots, block_len, width = tokens.shape
+    count = slots * block_len
+    pairs = width // PAIR
+    shape = jax.ShapeDtypeStruct
+    up_half = up_half.reshape(6, 4, width // 4, 256)
+    outs = [
+        shape(tokens.shape, WIDE),
+        shape((width // 16, 4 * width), WIDE),
+        shape((4 * width // 16, width), WIDE),
+        shape((width // 16, width), WIDE),
+        shape((width // 16, 3 * width), WIDE),
+        shape((16, width), WIDE),
+    ]
+    low = lambda *dims: pltpu.VMEM(dims, LOW)
+    wide = lambda *dims: pltpu.VMEM(dims, WIDE)
+    dma = pltpu.SemaphoreType.DMA
+    vmem = pl.BlockSpec(memory_space=pltpu.VMEM)
+    anywhere = pl.BlockSpec(memory_space=pltpu.HBM)
+    held = (resid_grad, mixer, qkv, edges, state_in, normed, weights, vectors, up_half, down_half)
+
+    def stages(lead, rows, columns):
+        return [
+            low(lead, 2, 4, rows, columns), low(lead, 4, rows, columns),
+            low(lead, 3, rows, columns), wide(lead, 2, rows, columns),
+        ]
+
+    return pl.pallas_call(
+        back_kernel,
+        out_shape=outs,
+        in_specs=[anywhere] * 9 + [vmem] + [anywhere] * 2,
+        out_specs=[anywhere] + [vmem] * 5,
+        scratch_shapes=[pltpu.VMEM(array.shape, array.dtype) for array in held]
+        + [
+            wide(slots, block_len + 8, width),
+            low(count, width),
+            low(slots, block_len, width),
+            low(3, slots, block_len, width),
+            wide(slots, block_len + 8, width),
+            low(width, count),
+            low(pairs, slots, PAIR, PAIR),
+            low(pairs, slots, PAIR, PAIR),
+            low(4, width // 4, width),
+            low(4, width // 4, width // 2),
+            low(pairs, 2, 4, width // 4, PAIR),
+            low(pairs, 4, width // 4, PAIR),
+            low(4, width // 4, width // 2),
+        ]
+        + stages(6, 48, 256) + stages(3, 64, 384) + stages(2, 48, 384) + stages(6, 48, PAIR)
+        + [
+            wide(16, width),
+            wide(3, 16, width),
+            wide(6, 16, width),
+            dma((17, 7)),
+            dma((17, 7)),
+            dma((11,)),
+            dma((2,)),
+            dma((4,)),
+            dma((4,)),
+            dma((6,)),
+            dma((6,)),
+            dma((6,)),
+            dma((6,)),
+        ],
+        compiler_params=pltpu.CompilerParams(
+            collective_id=1, has_side_effects=True, vmem_limit_bytes=63 * MIB
+        ),
+        name="backward_reduce",
+    )(
+        resid_grad, mixer, qkv, edges, state_in, normed, tokens.reshape(count, width), weights, vectors,
+        two_sums, up_half, down_half,
+    )
 
 
 def from_behind(value, axis, steps):
@@ -66,7 +1282,7 @@
     )
 
 
-def local(
+def general(
     tokens,
     ln1_gain,
     ln1_bias,
@@ -263,6 +1479,46 @@
     )
 
 
+def near(
+    tokens,
+    ln1_gain,
+    ln1_bias,
+    qkv_weight,
+    shift_taps,
+    decay_rates,
+    out_weight,
+    ln2_gain,
+    ln2_bias,
+    up_weight,
+    down_weight,
+    lengths,
+    out_grad,
+):
+    width = tokens.shape[2]
+    own = ln1_gain.shape[0]
+    packed = jnp.concatenate(
+        [
+            jnp.stack([ln1_gain, ln1_bias, decay_rates, ln2_gain, ln2_bias]),
+            shift_taps,
+            jnp.zeros((7, own), LOW),
+        ],
+        axis=0,
+    )
+    start = lax.axis_index("dp") * own
+    packed = lax.dynamic_update_slice(jnp.zeros((16, width), LOW), packed, (0, start))
+    (
+        mixed, normed, qkv, edges, state_in, mixer, resid_grad, weights, vectors, two_sums, up_half, down_half,
+    ) = front(packed, qkv_weight, out_weight, up_weight, down_weight, tokens, out_grad, lengths)
+    input_grad, up_sum, down_sum, out_sum, qkv_sum, small = back(
+        resid_grad, mixer, qkv, edges, state_in, normed, tokens, weights, vectors, two_sums, up_half, down_half,
+    )
+    small = lax.dynamic_slice(small, (0, start), (16, own))
+    return (
+        mixed, input_grad, small[0], small[1], qkv_sum, small[3:7], small[2], out_sum, small[8], small[9],
+        up_sum, down_sum,
+    )
+
+
 def solution(mesh):
     in_specs = (
         P("dp", "seq", None),
@@ -293,4 +1549,5 @@
         P("dp", None),
         P("dp", None),
     )
+    local = near if dict(mesh.shape) == {"dp": 16, "seq": 2} else general
     return jax.shard_map(local, mesh=mesh, in_specs=in_specs, out_specs=out_specs, check_vma=False)

time: 1190 us -> 221 us (0.19)
  waiting for transfers between devices: 687 us -> 0 us
  Pallas kernels: 0 us -> 207 us
  blocking collectives: 193 us -> 0 us
  matrix products: 192 us -> 0 us
  local copies, waits for them, and re-layouts: 52.4 us -> 12.6 us
  other arithmetic: 38.3 us -> 0 us
  between operations: 16.9 us -> 0.7 us
    reduce_scatter x4 -> x0, waiting for transfers between devices: 538 us -> none  [the longest x1 177 us: local(): lax.psum_scatter(up_grad, 'dp', scatter_dimension=0, tiled=True)]
    pallas_call x0 -> x2, Pallas kernels: none -> 207 us  [the longest x1 111 us: front(): pl.pallas_call(front_kernel, out_shape=outs, in_specs=[pl.BlockSpec(memor...]
    dot_general x24 -> x0, matrix products: 192 us -> none  [the longest x4 38.6 us: back_product(): lax.dot_general(grad_rows, weight, (((1,), (1,)), ((), ())), preferred_el...]
    unnamed x2 -> x0, blocking collectives: 154 us -> none
    all_gather x4 -> x0, waiting for transfers between devices: 92.6 us -> none  [the longest x1 70.5 us: local(): lax.all_gather(down_weight, 'dp', axis=0, tiled=True)]
    unnamed x11 -> x0, waiting for transfers between devices: 38.3 us -> none
    all_gather x1 -> x0, blocking collectives: 35.5 us -> none  [local(): lax.all_gather(shift_taps, 'dp', axis=1, tiled=True)]
    psum x1 -> x0, waiting for transfers between devices: 18.5 us -> none  [local(): lax.psum((reduced[0], reduced[1], reduced[2], reduced[3], reduced[4], red...]
  transfers between devices with their start and end apart: 14 -> 0, of which waited for: 8 -> 0; matrix products, arithmetic and copies ran while one was open for 16% -> 0% of each run, Pallas kernels for 0% -> 0%
where the time goes in v2:
time: 221 us
  Pallas kernels  207 us (94%)
  local copies, waits for them, and re-layouts  12.6 us (6%)
    pallas_call x1, Pallas kernels, front(): pl.pallas_call(front_kernel, out_shape=outs, in_specs=[pl.BlockSpec(memor...  111 us
    pallas_call x1, Pallas kernels, back(): pl.pallas_call(back_kernel, out_shape=outs, in_specs=[anywhere] * 9 + [vm...  96.4 us
    unnamed x18, local copies, waits for them, and re-layouts  7.99 us

profile of v2, /device:TPU:0, one launch (start us, length us, event | category | flops | bytes accessed | tf_op | source)
XLA Modules:
  0.0 220.6 jit_solution(12774184250199847140)
XLA Ops:
  0.7 1.6 concatenate.3
  2.2 0.2 dynamic_update_slice.3.packed
  2.4 0.0 copy-start.5
  2.4 0.6 copy-done.5
  3.0 110.9 %gather_forward_ffn.1 = (bf16[2,512,768]{2,1,0:T(8,128)(2,1)}, bf16[1024,768]{1,0:T(8,128)(2,1)}, bf16[3,2,512,768]{3,2,1,0:T(8,128)(2,1)}, bf16[2,16,768]{2,1,0...) custom-call(s32[2]{0:T(128)} %lengths.1, ...), custom_call_target="tpu_custom_call" | custom-call | tf_op jit(solution)/shard_map/gather_forward_ffn/pallas_call | solution.py:631
  113.9 96.4 %backward_reduce.1 = (f32[2,512,768]{2,1,0:T(8,128)}, f32[48,3072]{1,0:T(8,128)}, f32[192,768]{1,0:T(8,128)}, f32[48,768]{1,0:T(8,128)}, f32[48,2304]{1,0:T(8,128)}, /*index=5*/f32[16,768]{1,0:T(8,128)}) custom-call(f32[2,512,768]{2,1,0:T(8,128)} %get-tuple-element.31.resid_grad_in, bf16[1024,768]{1,0:T(8,128)(2,1)} %get-tuple-element.32.mixer_in, ...), custom_call_target="tpu_custom_call" | custom-call | tf_op jit(solution)/shard_map/backward_reduce/pallas_call | solution.py:1182
  210.3 0.0 copy-start
  210.3 1.5 dynamic-slice_bitcast_fusion
  211.8 1.3 dynamic-slice.2
  213.2 2.7 %copy.32 = bf16[2,512,768]{2,1,0:T(8,128)(2,1)} copy(bf16[2,512,768]{2,1,0:T(8,128)(2,1)} %get-tuple-element.65) | data formatting | bytes 3145728
  215.8 0.0 copy-done
  215.8 0.0 copy-start.3
  215.8 0.0 copy-start.4
  215.8 0.0 copy-start.2
  215.8 1.7 copy.33
  217.5 0.0 copy-done.3
  217.5 0.0 copy-start.1
  217.5 0.8 copy.34
  218.3 0.0 copy-done.4
  218.3 0.7 copy.35
  218.9 0.0 copy-done.2
  218.9 0.8 copy.36
  219.8 0.0 copy-done.1
  219.8 0.8 copy.37
  (2 shorter events, 0.0 us)
Async XLA Ops:
  2.4 0.6 copy-start.5
  210.3 5.5 %copy-start = (f32[2,512,768]{2,1,0:T(8,128)S(1)}, f32[2,512,768]{2,1,0:T(8,128)}, u32[]{:S(2)}) copy-start(f32[2,512,768]{2,1,0:T(8,128)} %get-tuple-element.66) | copy-start | bytes 9437188
  215.8 1.7 copy-start.3
  215.8 2.4 %copy-start.4 = (f32[48,768]{1,0:T(8,128)S(1)}, f32[48,768]{1,0:T(8,128)}, u32[]{:S(2)}) copy-start(f32[48,768]{1,0:T(8,128)} %get-tuple-element.72) | copy-start | bytes 442372
  215.8 3.1 %copy-start.2 = (f32[48,3072]{1,0:T(8,128)S(1)}, f32[48,3072]{1,0:T(8,128)}, u32[]{:S(2)}) copy-start(f32[48,3072]{1,0:T(8,128)} %get-tuple-element.75) | copy-start | bytes 1769476
  217.5 2.2 %copy-start.1 = (f32[192,768]{1,0:T(8,128)S(1)}, f32[192,768]{1,0:T(8,128)}, u32[]{:S(2)}) copy-start(f32[192,768]{1,0:T(8,128)} %get-tuple-element.76) | copy-start | bytes 1769476

commit v3 on v2

--- a/solution.py
+++ b/solution.py
@@ -72,9 +72,9 @@
 
 
 class Unit:
-    def __init__(self, shard, buffer, rows, lead=None, start=0, width=None, shared=False):
-        self.shard, self.buffer, self.rows, self.lead = shard, buffer, rows, lead
-        self.start, self.width, self.shared = start, width, shared
+    def __init__(self, shard, buffer, rows, tiles=None, start=0, width=None, shared=False, plane=False):
+        self.shard, self.buffer, self.rows, self.tiles = shard, buffer, rows, tiles
+        self.start, self.width, self.shared, self.plane = start, width, shared, plane
 
     def columns(self, side):
         if self.shared:
@@ -82,88 +82,119 @@
         return part(self.start + side * (self.width // 2), self.width // 2, 128)
 
     def own(self, side):
-        row, columns = self.shard[1], self.shard[2]
         if self.shared:
             return self.shard[0]
-        return self.shard[0].at[
-            pl.ds(row, self.rows), part(columns + side * (self.width // 2), self.width // 2, 128)
-        ]
+        columns = part(self.shard[1] + side * (self.width // 2), self.width // 2, 128)
+        if self.tiles:
+            return self.shard[0].at[pl.ds(*self.tiles), :, columns]
+        return self.shard[0].at[:, columns]
+
+    def at(self, z, rows, columns):
+        if self.tiles:
+            return self.buffer.at[pl.ds(*self.tiles), z, rows, columns]
+        return self.buffer.at[z, rows, columns]
 
     def slab(self, spot, columns):
-        rows = part(spot * self.rows, self.rows, 16)
-        if self.lead is None:
-            return self.buffer.at[:, rows, columns]
-        return self.buffer.at[pl.ds(self.lead, 4), rows, columns]
+        return self.at(slice(None), part(spot * self.rows, self.rows, 16), columns)
+
+    def floor(self, z, columns):
+        return self.at(z, slice(None), columns)
 
     def block(self, z, spot, columns):
-        rows = part(spot * self.rows, self.rows, 16)
-        return self.buffer.at[z if self.lead is None else self.lead + z, rows, columns]
+        return self.at(z, part(spot * self.rows, self.rows, 16), columns)
+
+
+class Script:
+    def __init__(self, events):
+        self.events, self.done, self.held = events, 0, set()
+
+    def take(self, count):
+        chosen = []
+        while len(chosen) < count and self.done < len(self.events):
+            which, event = self.events[self.done]
+            if which in self.held:
+                break
+            chosen.append(event)
+            self.done += 1
+        return chosen
+
+    def tick(self, count=1000):
+        for event in self.take(count):
+            event()
+
+    def points(self, trips, count, each=1, release=None):
+        chosen = []
+        for trip in range(trips):
+            if release is not None:
+                self.held -= release(trip)
+            for _ in range(count):
+                chosen.append(self.take(each))
+
+        def run(index, point):
+            for trip in range(trips):
+                events = chosen[trip * count + point]
+                if events:
+                    @pl.when(index == trip)
+                    def _(events=events):
+                        for event in events:
+                            event()
+
+        return run
 
 
 class Gather:
     def __init__(self, place, units, send_sem, recv_sem, local_sem):
         self.place, self.units = place, units
         self.send_sem, self.recv_sem, self.local_sem = send_sem, recv_sem, local_sem
-        self.events = []
+        self.script = Script([])
         self.ready = {}
+        events = self.script.events
         count = len(units)
         for turn in range(count + 2):
-            if turn < count:
-                self.events.append(functools.partial(self.after_z, turn))
-            if 1 <= turn < count + 1:
-                self.events.append(functools.partial(self.after_a, turn - 1))
-            if 2 <= turn:
-                self.events.append(functools.partial(self.after_b, turn - 2))
-                self.ready[turn - 2] = len(self.events)
-        self.done = 0
-
-    def tick(self, count=1):
-        for event in self.events[self.done : self.done + count]:
-            event()
-        self.done = min(self.done + count, len(self.events))
-
-    def spread(self, index, trips, each):
-        for trip in range(trips):
-            chosen = self.events[self.done : self.done + each]
-            self.done += len(chosen)
-            if chosen:
-                @pl.when(index == trip)
-                def _(chosen=chosen):
-                    for event in chosen:
-                        event()
+            for lag, step in enumerate((self.one, self.two, self.three)):
+                if 0 <= turn - lag < count:
+                    which = ORDER[turn - lag]
+                    events.append((which, functools.partial(step, which)))
+                    self.ready[which] = len(events)
 
     def need(self, which):
-        self.tick(max(0, self.ready[which] - self.done))
+        self.script.tick(max(0, self.ready[which] - self.script.done))
         self.land(which)
 
     def land(self, which):
-        unit = self.units[which]
+        unit, place = self.units[which], self.place
         if unit.shared:
             return
-        other = unit.columns(1 - self.place.core)
+        other = unit.columns(1 - place.core)
         for slot, (da, db) in enumerate(((0, 0), (1, 0), (0, 1), (1, 1))):
-            window = unit.slab(self.place.sibling_spot(da, db), other)
+            if unit.plane:
+                window = unit.floor((place.z + slot) % 4, other)
+            else:
+                window = unit.slab(place.sibling_spot(da, db), other)
             pltpu.make_async_copy(window, window, self.recv_sem.at[which, 6 + slot]).wait()
 
     def copy(self, which, slot):
         unit, place = self.units[which], self.place
         mine = unit.columns(place.core)
-        if slot < 3:
-            step = (slot + 1, 0, 0)
-            source = unit.own(place.core)
-            target = unit.block(place.z, place.spot(0, 0), mine)
-            landing = 2 - slot
-            device = place.peer(*step)
+        landing = slot
+        if slot >= 6:
+            device = place.sibling()
+        elif unit.plane:
+            device = place.peer(*((0, 1, 0), (0, 0, 1), (0, 0, 1), (1, 0, 0), (2, 0, 0), (3, 0, 0))[slot])
+            landing = 8 - slot if slot >= 3 else slot
         else:
-            da, db = {3: (0, 0), 4: (0, 0), 5: (1, 0), 6: (0, 0), 7: (1, 0), 8: (0, 1), 9: (1, 1)}[slot]
+            device = place.peer(*((1, 0, 0), (2, 0, 0), (3, 0, 0), (0, 1, 0), (0, 0, 1), (0, 0, 1))[slot])
+            landing = 2 - slot if slot < 3 else slot
+        if unit.plane and slot < 3:
+            target = unit.block(place.z, place.spot(1 if slot == 2 else 0, 0), mine)
+            source = target if slot == 2 else unit.own(place.core)
+        elif unit.plane:
+            source = target = unit.floor((place.z + max(0, slot - 6)) % 4, mine)
+        elif slot < 3:
+            source, target = unit.own(place.core), unit.block(place.z, place.spot(0, 0), mine)
+        else:
+            da, db = ((0, 0), (0, 0), (1, 0), (0, 0), (1, 0), (0, 1), (1, 1))[slot - 3]
             source = target = unit.slab(place.spot(da, db), mine)
-            landing = slot
-            if slot == 3:
-                device = place.peer(0, 1, 0)
-            elif slot < 6:
-                device = place.peer(0, 0, 1)
-            else:
-                device = place.sibling()
         return remote(
             source, target, self.send_sem.at[which, slot], self.recv_sem.at[which, landing], device
         )
@@ -178,41 +209,56 @@
 
     def start(self, which):
         self.stay(which).start()
-        for slot in range(3):
+        for slot in range(2 if self.units[which].plane else 3):
             self.copy(which, slot).start()
 
     def arrive(self, which, slot):
         unit, place = self.units[which], self.place
         mine = unit.columns(place.core)
-        if slot < 3:
+        if unit.plane and slot < 3:
+            window = unit.block(place.z, place.spot(*((1, 0), (0, 1), (1, 1))[slot]), mine)
+        elif unit.plane:
+            window = unit.floor((place.z + slot - 2) % 4, mine)
+        elif slot < 3:
             window = unit.block((place.z + slot + 1) % 4, place.spot(0, 0), mine)
         else:
-            da, db = {3: (1, 0), 4: (0, 1), 5: (1, 1)}[slot]
-            window = unit.slab(place.spot(da, db), mine)
+            window = unit.slab(place.spot(*((1, 0), (0, 1), (1, 1))[slot - 3]), mine)
         pltpu.make_async_copy(window, window, self.recv_sem.at[which, slot]).wait()
 
-    def pass_on(self, which, slot):
-        if not self.units[which].shared:
-            self.copy(which, slot).start()
-
-    def after_z(self, which):
+    def send(self, which, *slots):
+        for slot in slots:
+            if slot < 6 or not self.units[which].shared:
+                self.copy(which, slot).start()
+
+    def one(self, which):
         self.stay(which).wait()
+        if self.units[which].plane:
+            self.arrive(which, 0)
+            self.send(which, 2)
+            return
         for slot in range(3):
             self.arrive(which, slot)
-        self.copy(which, 3).start()
-        self.copy(which, 4).start()
-        self.pass_on(which, 6)
-
-    def after_a(self, which):
+        self.send(which, 3, 4, 6)
+
+    def two(self, which):
+        if self.units[which].plane:
+            self.arrive(which, 1)
+            self.arrive(which, 2)
+            self.send(which, 3, 4, 5, 6)
+            return
         self.arrive(which, 3)
-        self.copy(which, 5).start()
-        self.pass_on(which, 7)
-
-    def after_b(self, which):
+        self.send(which, 5, 7)
+
+    def three(self, which):
+        if self.units[which].plane:
+            for slot in range(3, 6):
+                self.arrive(which, slot)
+                self.send(which, slot + 4)
+            return
         self.arrive(which, 4)
-        self.pass_on(which, 8)
+        self.send(which, 8)
         self.arrive(which, 5)
-        self.pass_on(which, 9)
+        self.send(which, 9)
 
     def drain(self):
         for which, unit in enumerate(self.units):
@@ -290,35 +336,45 @@
     return total
 
 
+LOTS = 6
+
+
 def hidden_order(shard):
+    size = shard.shape[1] // (16 * LOTS)
     pieces = [
-        shard[:, device * 192 + lot * 64 : device * 192 + lot * 64 + 64]
-        for lot in range(3)
+        shard[:, (device * LOTS + lot) * size : (device * LOTS + lot + 1) * size]
+        for lot in range(LOTS)
         for device in range(16)
     ]
     return jnp.concatenate(pieces, axis=1)
 
 
 def hidden_disorder(columns):
+    size = columns.shape[1] // (16 * LOTS)
     pieces = [
-        columns[:, lot * 1024 + device * 64 : lot * 1024 + device * 64 + 64]
+        columns[:, (lot * 16 + device) * size : (lot * 16 + device + 1) * size]
         for device in range(16)
-        for lot in range(3)
+        for lot in range(LOTS)
     ]
     return jnp.concatenate(pieces, axis=1)
 
 
 VEC, KEY, VALUE, QUERY, OUT, DOWN, UP = range(7)
+GROUPS = ((0, 2), (2, 2), (4, 1), (5, 1))
+EARLY = 4
+ORDER = tuple(range(13))
+APART = 3
 
 
 def front_kernel(
     lengths, packed, qkv_shard, out_shard, up_shard, down_shard, tokens_in, cotangent_in,
     mixed_out, normed_out, qkv_out, edges_out, state_out, mixer_out, resid_grad_out, weights_out,
-    vectors_out, sums_out, up_out, down_out,
+    vectors_out, sums_out, up_out, down_out, up_b_out, down_b_out,
     vec_all, weights, up_all, down_all, up_own, tokens, grad_low, normed, qkv, edges, state_in,
-    state_send, mixer, resid, normed_two, normed_turned, keys, summed, mixed, vectors, sums,
-    up_stage, down_stage, up_half, down_half,
+    state_send, mixer, resid, normed_turned, keys, summed, vectors, sums,
+    up_stage, down_stage, up_half, down_half, up_b, down_b,
     send_sem, recv_sem, local_sem, load_sem, save_sem, pair_send, pair_recv, tile_send, tile_recv,
+    early_send, early_recv,
 ):
     slots, block_len, width = tokens.shape
     pairs = width // PAIR
@@ -328,16 +384,18 @@
     core = place.core
     first = core == 0
     queries, key_rows, values = qkv.at[0], qkv.at[1], qkv.at[2]
+    normed_two, mixer_view = normed, mixer
 
     def load(slot, source, target):
         return pltpu.make_async_copy(source, target, load_sem.at[slot])
 
     def save(slot):
         source, target = (
-            (mixed, mixed_out), (normed, normed_out), (qkv, qkv_out), (edges, edges_out),
+            (mixer_view, mixed_out), (normed, normed_out), (qkv, qkv_out), (edges, edges_out),
             (state_in, state_out), (mixer, mixer_out), (keys.at[:, pl.ds(0, block_len)], resid_grad_out),
-            (weights, weights_out), (vectors, vectors_out), (sums, sums_out), (up_half, up_out),
-            (down_half, down_out),
+            (weights, weights_out), (vectors, vectors_out), (sums, sums_out),
+            (up_half.at[pl.ds(EARLY, tiles - EARLY)], up_out),
+            (down_half.at[pl.ds(EARLY, tiles - EARLY)], down_out), (up_b, up_b_out), (down_b, down_b_out),
         )[slot]
         return pltpu.make_async_copy(source, target, save_sem.at[slot])
 
@@ -346,15 +404,15 @@
     load(2, cotangent_in, grad_low).start()
     enter(place)
     units = [
-        Unit((packed, 0, 0), vec_all, 16, shared=True),
-        Unit((qkv_shard, 0, width), weights.at[1], 48, width=width),
-        Unit((qkv_shard, 0, 2 * width), weights.at[2], 48, width=width),
-        Unit((qkv_shard, 0, 0), weights.at[0], 48, width=width),
-        Unit((out_shard, 0, 0), weights.at[3], 48, width=width),
+        Unit((packed, 0), vec_all, 16, shared=True),
+        Unit((qkv_shard, width), weights.at[1], 48, width=width),
+        Unit((qkv_shard, 2 * width), weights.at[2], 48, width=width),
+        Unit((qkv_shard, 0), weights.at[0], 48, width=width),
+        Unit((out_shard, 0), weights.at[3], 48, width=width),
     ]
-    for lot in range(3):
-        units.append(Unit((down_shard, lot * 64, 0), down_all, 64, lead=4 * lot, width=width))
-        units.append(Unit((up_own, 0, lot * 1024), up_all, 48, start=lot * 1024, width=1024))
+    for lot, count in GROUPS:
+        units.append(Unit((down_shard, 0), down_all, 32, tiles=(lot, count), width=width))
+        units.append(Unit((up_own, lot * 512), up_all, 48, start=lot * 512, width=count * 512))
     gather = Gather(place, units, send_sem, recv_sem, local_sem)
     for which in range(5):
         gather.start(which)
@@ -436,10 +494,12 @@
         lax.fori_loop(0, pairs, fresh, 0)
         state_copy.start()
 
-    gather.tick(2)
+    gather.script.tick(2)
+
+    spread_within = gather.script.points(pairs, 1)
 
     def within(pair, carry):
-        gather.spread(pair, pairs, TICKS_WITHIN)
+        spread_within(pair, 0)
         window = lanes(pair)
         rate = vectors[ROW_RATE : ROW_RATE + 1, window]
         taps = vectors[ROW_TAPS : ROW_TAPS + 4, window]
@@ -492,8 +552,10 @@
     gain_two, bias_two = vectors[3:4], vectors[4:5]
     for slot in range(slots):
         rows = slice(slot * block_len, (slot + 1) * block_len)
-        mixer[rows] = summed[slot].astype(LOW)
-        total = tokens[slot].astype(WIDE) + nn(mixer[rows], weight(3))
+        if slot == 0:
+            save(1).wait()
+        mixer[slot] = summed[slot].astype(LOW)
+        total = tokens[slot].astype(WIDE) + nn(mixer[slot], weight(3))
         resid[slot] = total
         summed[slot] = total
         hat, _ = normalize(total)
@@ -509,7 +571,7 @@
         other = 1 - core
         return (
             remote(
-                up_stage.at[slot, :, part(other * 256, 256, 128)],
+                up_stage.at[slot, :, :, part(other * 256, 256, 128)],
                 up_half.at[tile],
                 tile_send.at[tile, 0],
                 tile_recv.at[tile, 0],
@@ -517,7 +579,7 @@
             ),
             remote(
                 down_stage.at[slot, :, :, part(other * 384, 384, 128)],
-                down_half.at[pl.ds(2 * tile, 2)],
+                down_half.at[tile],
                 tile_send.at[tile, 1],
                 tile_recv.at[tile, 1],
                 place.sibling(),
@@ -528,20 +590,28 @@
         for copy in tile_copies(tile):
             copy.wait_recv()
         slot = tile % 2
-        up_half[tile] = up_half[tile] + up_stage[slot, :, part(core * 256, 256, 128)]
-        window = pl.ds(2 * tile, 2)
-        down_half[window] = down_half[window] + down_stage[slot, :, :, part(core * 384, 384, 128)]
+        up_half[tile] = up_half[tile] + up_stage[slot, :, :, part(core * 256, 256, 128)]
+        down_half[tile] = down_half[tile] + down_stage[slot, :, :, part(core * 384, 384, 128)]
+
+    shares = [
+        Share(up_half.at[k], up_half.at[k], up_b.at[k], None, None, None, 48) for k in range(EARLY)
+    ] + [
+        Share(down_half.at[k], down_half.at[k], down_b.at[k], None, None, None, 32) for k in range(EARLY)
+    ]
+    early = Reduction(place, shares, early_send, early_recv)
+    spread = gather.script.points(tiles, 3)
 
     def ffn_tile(tile, carry):
-        for lot in range(1, 3):
-            @pl.when(tile == 2 * lot)
-            def _(lot=lot):
-                gather.land(DOWN + 2 * lot)
-                gather.land(UP + 2 * lot)
-
+        for group in range(1, len(GROUPS)):
+            @pl.when(tile == GROUPS[group][0])
+            def _(group=group):
+                gather.land(DOWN + 2 * group)
+                gather.land(UP + 2 * group)
+
+        spread(tile, 0)
         columns = part(tile * 512, 512, 512)
         up = up_all[:, :, columns].reshape(width, 512)
-        down = down_all[pl.ds(2 * tile, 2)].reshape(512, width)
+        down = down_all[tile].reshape(512, width)
         cotangent = grad_low[...].reshape(slots * block_len, width)
         pre = nn(normed_two[...], up)
         wide = nt(cotangent, down)
@@ -553,33 +623,42 @@
         )
         act = (pre * half).astype(LOW)
         back = (wide * slope).astype(LOW)
+        spread(tile, 1)
+
+        @pl.when(tile >= 1)
+        def _():
+            merge(tile - 1)
+
+        for k in range(EARLY):
+            @pl.when(tile == k + 1)
+            def _(k=k):
+                early.start(k)
+                early.start(EARLY + k)
+
         for slot in range(slots):
             rows = slice(slot * block_len, (slot + 1) * block_len)
             summed[slot] += nn(act[rows], down)
             keys[slot, 0:block_len] += nt(back[rows], up)
         turn = tile % 2
+        spread(tile, 2)
 
         @pl.when(tile >= 2)
         def _():
             for copy in tile_copies(tile - 2):
                 copy.wait_send()
 
-        gather.spread(tile, tiles, TICKS_FFN)
-        up_stage[turn] = nn(normed_turned[...], back).astype(LOW)
-        down_stage[turn] = tn(act, cotangent).astype(LOW).reshape(2, 256, width)
+        up_stage[turn] = nn(normed_turned[...], back).astype(LOW).reshape(4, width // 4, 512)
+        down_stage[turn] = tn(act, cotangent).astype(LOW).reshape(4, 128, width)
         for copy in tile_copies(tile):
             copy.start()
-
-        @pl.when(tile >= 1)
-        def _():
-            merge(tile - 1)
-
         return carry
 
     lax.fori_loop(0, tiles, ffn_tile, 0)
     sums[...] = jnp.zeros_like(sums)
     for slot in range(slots):
-        mixed[slot] = summed[slot].astype(LOW)
+        if slot == 0:
+            save(5).wait()
+        mixer[slot] = summed[slot].astype(LOW)
         hat, scale = normalize(resid[slot])
         grad = keys[slot, 0:block_len]
         sums[0:1] += jnp.sum(grad * hat, axis=0, keepdims=True)
@@ -588,19 +667,22 @@
     save(0).start()
     save(6).start()
     save(9).start()
+    for k in range(EARLY):
+        early.merge_b(k)
+        early.merge_b(EARLY + k)
+    save(12).start()
+    save(13).start()
     merge(tiles - 1)
     save(10).start()
     save(11).start()
     for tile in (tiles - 2, tiles - 1):
         for copy in tile_copies(tile):
             copy.wait_send()
-    gather.tick(len(gather.events))
+    gather.script.tick()
     gather.drain()
-    for slot in range(12):
+    early.drain()
+    for slot in (0, 2, 3, 4, 6, 7, 8, 9, 10, 11, 12, 13):
         save(slot).wait()
-
-
-TICKS_WITHIN, TICKS_FFN = 1, 3
 
 
 def front(packed, qkv_weight, out_weight, up_weight, down_weight, tokens, cotangent, lengths):
@@ -616,13 +698,15 @@
         shape((3, slots, block_len, width), LOW),
         shape((slots, 16, width), LOW),
         shape((pairs, slots, PAIR, PAIR), WIDE),
-        shape((count, width), LOW),
+        shape(tokens.shape, LOW),
         shape(tokens.shape, WIDE),
         shape((4, 4, width // 4, width), LOW),
         shape((16, width), WIDE),
         shape((8, width), WIDE),
-        shape((tiles, width, 256), LOW),
-        shape((2 * tiles, 256, width // 2), LOW),
+        shape((tiles - EARLY, 4, width // 4, 256), LOW),
+        shape((tiles - EARLY, 4, 128, width // 2), LOW),
+        shape((EARLY, 2, 4, width // 16, 256), LOW),
+        shape((EARLY, 2, 4, 32, width // 2), LOW),
     ]
     vmem = lambda *dims: pltpu.VMEM(dims, LOW)
     wide = lambda *dims: pltpu.VMEM(dims, WIDE)
@@ -637,7 +721,7 @@
             vmem(4, 64, width),
             vmem(4, 4, width // 4, width),
             vmem(4, width // 4, hidden),
-            vmem(12, 256, width),
+            vmem(tiles, 4, 128, width),
             vmem(width // 16, hidden),
             vmem(slots, block_len, width),
             vmem(slots, block_len, width),
@@ -646,34 +730,39 @@
             vmem(slots, 16, width),
             wide(pairs, slots, PAIR, PAIR),
             wide(pairs, slots, PAIR, PAIR),
-            vmem(count, width),
+            vmem(slots, block_len, width),
             wide(slots, block_len, width),
-            vmem(count, width),
             vmem(width, count),
             wide(slots, block_len + 8, width),
             wide(slots, block_len, width),
-            vmem(slots, block_len, width),
             wide(16, width),
             wide(8, width),
-            vmem(2, width, 512),
-            vmem(2, 2, 256, width),
-            vmem(tiles, width, 256),
-            vmem(2 * tiles, 256, width // 2),
-            dma((11, 10)),
-            dma((11, 10)),
-            dma((11,)),
+            vmem(2, 4, width // 4, 512),
+            vmem(2, 4, 128, width),
+            vmem(tiles, 4, width // 4, 256),
+            vmem(tiles, 4, 128, width // 2),
+            vmem(EARLY, 2, 4, width // 16, 256),
+            vmem(EARLY, 2, 4, 32, width // 2),
+            dma((13, 10)),
+            dma((13, 10)),
+            dma((13,)),
             dma((3,)),
-            dma((12,)),
+            dma((14,)),
             dma((2,)),
             dma((2,)),
             dma((tiles, 2)),
             dma((tiles, 2)),
+            dma((2 * EARLY, 2)),
+            dma((2 * EARLY, 2)),
         ],
         compiler_params=pltpu.CompilerParams(
             collective_id=0, has_side_effects=True, vmem_limit_bytes=63 * MIB
         ),
         name="gather_forward_ffn",
-    )(lengths, packed, qkv_weight, out_weight, up_weight, down_weight, tokens, cotangent)
+    )(
+        lengths, packed, qkv_weight, out_weight, up_weight, down_weight.reshape(tiles, 32, width), tokens,
+        cotangent,
+    )
 
 
 class Share:
@@ -710,6 +799,9 @@
         return remote(source, target, self.send_sem.at[which, slot], self.recv_sem.at[which, slot], device)
 
     def start(self, which):
+        if self.shares[which].source is None:
+            self.copy(which, 2).start()
+            return
         for slot in range(2):
             self.copy(which, slot).start()
 
@@ -721,7 +813,7 @@
             a = (place.a + da) % 2
             rows = part(place.spot(da, 0) * share.rows, share.rows, 16)
             share.from_b[a] = share.from_b[a] + share.own[:, rows]
-            if slot == 0:
+            if slot == 0 and share.from_a is not None:
                 self.copy(which, 2).start()
 
     def merge_a(self, which):
@@ -746,47 +838,31 @@
         pltpu.make_async_copy(other, other, self.recv_sem.at[which, 6]).wait()
 
     def drain(self):
-        for which in range(len(self.shares)):
-            for slot in range(7):
+        for which, share in enumerate(self.shares):
+            first = 2 if share.source is None else 0
+            for slot in range(first, 2 if share.from_a is None else 7):
                 self.copy(which, slot).wait_send()
 
-
-class Script:
-    def __init__(self, events):
-        self.events, self.done = events, 0
-
-    def tick(self, count):
-        for event in self.events[self.done : self.done + count]:
-            event()
-        self.done = min(self.done + count, len(self.events))
-
-    def spread(self, index, trips, each):
-        for trip in range(trips):
-            chosen = self.events[self.done : self.done + each]
-            self.done += len(chosen)
-            if chosen:
-                @pl.when(index == trip)
-                def _(chosen=chosen):
-                    for event in chosen:
-                        event()
-
-
-def staggered(reduction, which):
-    events = []
-    which = list(which)
-    for turn in range(len(which) + 2):
-        for lag, step in enumerate((reduction.merge_b, reduction.merge_a, reduction.finish)):
-            if 0 <= turn - lag < len(which):
-                events.append(functools.partial(step, which[turn - lag]))
-    return events
-
-
-UPS, DOWNS, OUTS, PAIRS, KEYS = 0, 6, 9, 10, 16
+    def events(self, order):
+        steps = []
+        for which in order:
+            own = [self.merge_b] if self.shares[which].source is not None else []
+            steps.append([functools.partial(f, which) for f in own + [self.merge_a, self.finish]])
+        events = []
+        for turn in range(len(steps) + 3 * APART):
+            for which in range(len(steps)):
+                step, rest = divmod(turn - which, APART)
+                if rest == 0 and 0 <= step < len(steps[which]):
+                    events.append((order[which], steps[which][step]))
+        return events
+
+
+UPS, DOWNS, OUTS, PAIRS, KEYS = 0, 6, 12, 13, 19
 
 
 def back_kernel(
     resid_grad_in, mixer_in, qkv_in, edges_in, state_in_in, normed_in, tokens_in, weights_in,
-    vectors_in, two_sums, up_in, down_in,
+    vectors_in, two_sums, up_in, down_in, up_b_in, down_b_in,
     input_grad_out, up_sum, down_sum, out_sum, qkv_sum, small_out,
     resid_grad, mixer, qkv, edges, state_in, normed, weights, vectors, up_half, down_half,
     keys, branch, back_rows, projected, key_back, normed_turned, state_send, state_grad,
@@ -794,7 +870,7 @@
     up_b, up_a, up_z, up_final, down_b, down_a, down_z, down_final, wide_b, wide_a, wide_z, wide_final,
     pair_b, pair_a, pair_z, pair_final, small, small_sums, small_from,
     send_sem, recv_sem, load_sem, save_sem, core_send, core_recv, pair_send, pair_recv,
-    small_send, small_recv,
+    small_send, small_recv, key_send, key_recv,
 ):
     slots, block_len, width = resid_grad.shape
     pairs = width // PAIR
@@ -807,50 +883,47 @@
     inputs = (
         (resid_grad_in, resid_grad), (weights_in, weights), (vectors_in, vectors), (qkv_in, qkv),
         (mixer_in, mixer), (edges_in, edges), (state_in_in, state_in), (normed_in, normed),
-        (up_in, up_half), (down_in, down_half), (tokens_in, mixer),
+        (up_in, up_half), (down_in, down_half), (up_b_in, up_b.at[pl.ds(0, EARLY)]),
+        (down_b_in, down_b.at[pl.ds(0, EARLY)]), (tokens_in, mixer),
     )
     LOAD_GRAD, LOAD_WEIGHTS, LOAD_VECTORS, LOAD_QKV, LOAD_MIXER, LOAD_EDGES, LOAD_STATE = range(7)
-    LOAD_NORMED, LOAD_UP, LOAD_DOWN, LOAD_TOKENS = range(7, 11)
+    LOAD_NORMED, LOAD_UP, LOAD_DOWN, LOAD_UP_B, LOAD_DOWN_B, LOAD_TOKENS = range(7, 13)
 
     def load(slot):
         return pltpu.make_async_copy(*inputs[slot], load_sem.at[slot])
 
-    for slot in range(LOAD_TOKENS):
+    for slot in (
+        LOAD_UP, LOAD_DOWN, LOAD_UP_B, LOAD_DOWN_B, LOAD_GRAD, LOAD_WEIGHTS, LOAD_VECTORS, LOAD_QKV,
+        LOAD_MIXER, LOAD_EDGES, LOAD_STATE, LOAD_NORMED,
+    ):
         load(slot).start()
     enter(place)
-    shares = [
-        Share(
-            up_in.at[k], up_half.at[k],
-            up_b.at[k], up_a.at[k], up_z.at[k], up_final.at[k], 48,
-        )
-        for k in range(6)
-    ]
-    shares += [
-        Share(
-            down_in.at[pl.ds(4 * k, 4)], down_half.at[pl.ds(4 * k, 4)],
-            down_b.at[k], down_a.at[k], down_z.at[k], down_final.at[k], 64,
-        )
-        for k in range(3)
-    ]
-    shares.append(
-        Share(out_half, out_half, wide_b.at[0], wide_a.at[0], wide_z.at[0], wide_final.at[0], 48)
-    )
-    shares += [
-        Share(
-            pair_half.at[k], pair_half.at[k], pair_b.at[k], pair_a.at[k], pair_z.at[k],
-            pair_final.at[k], 48,
-        )
-        for k in range(6)
-    ]
-    shares.append(
-        Share(key_half, key_half, wide_b.at[1], wide_a.at[1], wide_z.at[1], wide_final.at[1], 48)
-    )
+    tiles = EARLY + up_half.shape[0]
+
+    def tile_share(k, halves, from_b, from_a, from_z, final, rows):
+        own = None if k < EARLY else halves.at[k - EARLY]
+        return Share(own, own, from_b.at[k], from_a.at[k], from_z.at[k], final.at[k], rows)
+
+    def column_share(half, k):
+        return Share(half, half, wide_b.at[k], wide_a.at[k], wide_z.at[k], wide_final.at[k], 48)
+
+    def pair_share(half, k):
+        return Share(half, half, pair_b.at[k], pair_a.at[k], pair_z.at[k], pair_final.at[k], 48)
+
+    shares = [tile_share(k, up_half, up_b, up_a, up_z, up_final, 48) for k in range(tiles)]
+    shares += [tile_share(k, down_half, down_b, down_a, down_z, down_final, 32) for k in range(tiles)]
+    shares.append(column_share(out_half, 0))
+    shares += [pair_share(pair_half.at[k], k) for k in range(pairs)]
+    shares += [pair_share(key_half.at[k], pairs + k) for k in range(3)]
     reduction = Reduction(place, shares, send_sem, recv_sem)
-    for k in range(3):
-        reduction.start(UPS + 2 * k)
-        reduction.start(UPS + 2 * k + 1)
-        reduction.start(DOWNS + k)
-    script = Script(staggered(reduction, (0, 1, 6, 2, 3, 7, 4, 5, 8, 9)))
+    for slot in (LOAD_UP, LOAD_DOWN, LOAD_UP_B, LOAD_DOWN_B):
+        load(slot).wait()
+    order = [kind + k for k in range(tiles) for kind in (UPS, DOWNS)]
+    for which in order[2 * EARLY :] + order[: 2 * EARLY]:
+        reduction.start(which)
+    order += [OUTS, *range(PAIRS, PAIRS + pairs), *range(KEYS, KEYS + 3)]
+    script = Script(reduction.events(order))
+    script.held = {OUTS, *range(PAIRS, PAIRS + pairs), *range(KEYS, KEYS + 3)}
     spots = spots_of(block_len)
 
     load(LOAD_GRAD).wait()
@@ -880,20 +953,24 @@
         state_copy.start()
 
     load(LOAD_MIXER).wait()
-    load(LOAD_UP).wait()
-    load(LOAD_DOWN).wait()
     normed_turned[...] = mixer[...].T
     out_stage[...] = nn(normed_turned[...], branch[...]).astype(LOW).reshape(4, width // 4, width)
 
-    def halves(stage, half, sem):
-        window = part((1 - core) * (width // 2), width // 2, 128)
-        return remote(stage.at[:, :, window], half, core_send.at[sem], core_recv.at[sem], place.sibling())
-
-    def own_half(stage, half):
-        half[...] = half[...] + stage[:, :, part(core * (width // 2), width // 2, 128)]
-
     load(LOAD_TOKENS).start()
-    out_copy = halves(out_stage, out_half, 2)
+
+    def key_copy(k):
+        window = part((1 - core) * (width // 2) + k * PAIR, PAIR, 128)
+        return remote(
+            out_stage.at[:, :, window], key_half.at[k], key_send.at[k], key_recv.at[k], place.sibling()
+        )
+
+    out_copy = remote(
+        out_stage.at[:, :, part((1 - core) * (width // 2), width // 2, 128)],
+        out_half,
+        core_send.at[2],
+        core_recv.at[2],
+        place.sibling(),
+    )
     out_copy.start()
     load(LOAD_EDGES).wait()
     load(LOAD_STATE).wait()
@@ -903,8 +980,9 @@
         keys[slot, 0:8] = edges[slot].astype(WIDE)[8:16]
         keys[slot, 8:] = key_rows[slot].astype(WIDE)
     out_copy.wait_recv()
-    own_half(out_stage, out_half)
+    out_half[...] = out_half[...] + out_stage[:, :, part(core * (width // 2), width // 2, 128)]
     reduction.start(OUTS)
+    script.held -= {OUTS}
 
     @pl.when(second)
     def _():
@@ -925,8 +1003,12 @@
         pair_copy(pair).wait_recv()
         pair_half[pair] = pair_half[pair] + pair_stage[pair, core]
 
+    spread = script.points(
+        pairs, 2, TICKS_BACK, lambda trip: {PAIRS + trip - 2} if trip >= 2 else set()
+    )
+
     def back_pair(pair, carry):
-        script.spread(pair, pairs, TICKS_BACK)
+        spread(pair, 0)
         window = lanes(pair)
         rate = vectors[ROW_RATE : ROW_RATE + 1, window]
         taps = vectors[ROW_TAPS : ROW_TAPS + 4, window]
@@ -938,6 +1020,8 @@
         taps_grad = [jnp.zeros((1, PAIR), WIDE) for _ in range(4)]
         weight_grad = jnp.zeros((width, 2 * PAIR), WIDE)
         for slot in range(slots):
+            if slot == 1:
+                spread(pair, 1)
             query = queries[slot, :, window].astype(WIDE)
             key = shifted_keys(keys, slot, window, taps)
             value = values[slot, :, window]
@@ -1043,15 +1127,19 @@
         spill.start()
         key_back[:, block_len : block_len + 8] = jnp.zeros((slots, 8, width), WIDE)
 
-    script.tick(3)
     merge_pair(pairs - 1)
     reduction.start(PAIRS + pairs - 1)
+    script.held -= set(range(PAIRS, PAIRS + pairs))
+    out_copy.wait_send()
 
     @pl.when(first)
     def _():
         spill.wait_recv()
 
+    spread_keys = script.points(pairs, 1, 1)
+
     def key_pair(pair, carry):
+        spread_keys(pair, 0)
         window = lanes(pair)
         taps = vectors[ROW_TAPS : ROW_TAPS + 4, window]
         for slot in range(slots):
@@ -1063,25 +1151,26 @@
 
     lax.fori_loop(0, pairs, key_pair, 0)
     rows_all = projected[1].reshape(slots * block_len, width)
-    out_copy.wait_send()
     out_stage[...] = nn(normed_turned[...], rows_all).astype(LOW).reshape(4, width // 4, width)
-    key_copy = halves(out_stage, key_half, 3)
-    key_copy.start()
-    script.tick(len(script.events))
-    late = Script(staggered(reduction, (*range(PAIRS, PAIRS + pairs), KEYS)))
-    late.tick(3)
+    for k in range(3):
+        key_copy(k).start()
+    script.tick(3)
     load(LOAD_TOKENS).wait()
     gain = vectors[0:1]
-    key_copy.wait_recv()
-    own_half(out_stage, key_half)
-    reduction.start(KEYS)
     gain_sum = jnp.zeros((1, width), WIDE)
     bias_sum = jnp.zeros((1, width), WIDE)
     for slot in range(slots):
-        late.tick(4)
         grad = nt(projected[0, slot], weights[0].reshape(width, width))
         for third in range(1, 3):
             grad = grad + nt(projected[third, slot], weights[third].reshape(width, width))
+        if slot == 0:
+            for k in range(3):
+                key_copy(k).wait_recv()
+                window = part(core * (width // 2) + k * PAIR, PAIR, 128)
+                key_half[k] = key_half[k] + out_stage[:, :, window]
+                reduction.start(KEYS + k)
+            script.held.clear()
+        script.tick(4)
         hat, scale = normalize(mixer[slot * block_len : (slot + 1) * block_len].astype(WIDE))
         gain_sum = gain_sum + jnp.sum(grad * hat, axis=0, keepdims=True)
         bias_sum = bias_sum + jnp.sum(grad, axis=0, keepdims=True)
@@ -1089,6 +1178,7 @@
         pltpu.make_async_copy(
             resid_grad.at[slot], input_grad_out.at[slot], save_sem.at[slot]
         ).start()
+        script.tick(4)
     small[0:1], small[1:2] = gain_sum, bias_sum
     small[8:16] = two_sums[...]
 
@@ -1101,7 +1191,7 @@
 
     small_copy(0).start()
     for slot in range(3):
-        late.tick(2)
+        script.tick(2)
         small_copy(slot).wait_recv()
         before = small[...] if slot == 0 else small_sums[slot - 1]
         small_sums[slot] = before + small_from[slot]
@@ -1109,7 +1199,7 @@
             small_copy(slot + 1).start()
     for slot in range(3, 6):
         small_copy(slot).start()
-    late.tick(len(late.events))
+    script.tick()
     for slot in range(3, 6):
         small_copy(slot).wait_recv()
     small_from[2] = small_sums[2]
@@ -1121,12 +1211,14 @@
         reduction.land(which)
     ups = [up_final[tile, side] for tile in range(6) for side in range(2)]
     up_sum[...] = hidden_disorder(jnp.concatenate(ups, axis=1))
-    for lot in range(3):
-        for side in range(2):
-            down_sum[lot * 64 : lot * 64 + 64, side * 384 : side * 384 + 384] = down_final[lot, side]
     for side in range(2):
-        out_sum[:, side * 384 : side * 384 + 384] = wide_final[0, side]
-        qkv_sum[:, width + side * 384 : width + side * 384 + 384] = wide_final[1, side]
+        half = slice(side * 384, side * 384 + 384)
+        for tile in range(tiles):
+            down_sum[tile * 32 : tile * 32 + 32, half] = down_final[tile, side]
+        out_sum[:, half] = wide_final[0, side]
+        for k in range(3):
+            start = width + side * 384 + k * PAIR
+            qkv_sum[:, start : start + PAIR] = pair_final[pairs + k, side]
         for pair in range(pairs):
             start = 2 * width * side + pair * PAIR
             qkv_sum[:, start : start + PAIR] = pair_final[pair, side]
@@ -1135,7 +1227,8 @@
         small_copy(slot).wait_send()
     for pair in range(pairs):
         pair_copy(pair).wait_send()
-    key_copy.wait_send()
+    for k in range(3):
+        key_copy(k).wait_send()
 
     @pl.when(second)
     def _():
@@ -1147,17 +1240,16 @@
         ).wait()
 
 
-TICKS_BACK = 4
+TICKS_BACK = 2
 
 
 def back(
-    resid_grad, mixer, qkv, edges, state_in, normed, tokens, weights, vectors, two_sums, up_half, down_half,
+    resid_grad, mixer, qkv, edges, state_in, normed, tokens, weights, vectors, two_sums, up_half, down_half, up_b, down_b,
 ):
     slots, block_len, width = tokens.shape
     count = slots * block_len
     pairs = width // PAIR
     shape = jax.ShapeDtypeStruct
-    up_half = up_half.reshape(6, 4, width // 4, 256)
     outs = [
         shape(tokens.shape, WIDE),
         shape((width // 16, 4 * width), WIDE),
@@ -1171,7 +1263,8 @@
     dma = pltpu.SemaphoreType.DMA
     vmem = pl.BlockSpec(memory_space=pltpu.VMEM)
     anywhere = pl.BlockSpec(memory_space=pltpu.HBM)
-    held = (resid_grad, mixer, qkv, edges, state_in, normed, weights, vectors, up_half, down_half)
+    tiles = EARLY + up_half.shape[0]
+    held = (resid_grad, mixer.reshape(count, width), qkv, edges, state_in, normed, weights, vectors, up_half, down_half)
 
     def stages(lead, rows, columns):
         return [
@@ -1182,7 +1275,7 @@
     return pl.pallas_call(
         back_kernel,
         out_shape=outs,
-        in_specs=[anywhere] * 9 + [vmem] + [anywhere] * 2,
+        in_specs=[anywhere] * 9 + [vmem] + [anywhere] * 4,
         out_specs=[anywhere] + [vmem] * 5,
         scratch_shapes=[pltpu.VMEM(array.shape, array.dtype) for array in held]
         + [
@@ -1198,31 +1291,33 @@
             low(4, width // 4, width // 2),
             low(pairs, 2, 4, width // 4, PAIR),
             low(pairs, 4, width // 4, PAIR),
-            low(4, width // 4, width // 2),
+            low(3, 4, width // 4, PAIR),
         ]
-        + stages(6, 48, 256) + stages(3, 64, 384) + stages(2, 48, 384) + stages(6, 48, PAIR)
+        + stages(tiles, 48, 256) + stages(tiles, 32, 384) + stages(1, 48, 384) + stages(pairs + 3, 48, PAIR)
         + [
             wide(16, width),
             wide(3, 16, width),
             wide(6, 16, width),
-            dma((17, 7)),
-            dma((17, 7)),
-            dma((11,)),
+            dma((22, 7)),
+            dma((22, 7)),
+            dma((13,)),
             dma((2,)),
-            dma((4,)),
-            dma((4,)),
+            dma((3,)),
+            dma((3,)),
             dma((6,)),
             dma((6,)),
             dma((6,)),
             dma((6,)),
+            dma((3,)),
+            dma((3,)),
         ],
         compiler_params=pltpu.CompilerParams(
             collective_id=1, has_side_effects=True, vmem_limit_bytes=63 * MIB
         ),
         name="backward_reduce",
     )(
-        resid_grad, mixer, qkv, edges, state_in, normed, tokens.reshape(count, width), weights, vectors,
-        two_sums, up_half, down_half,
+        resid_grad, mixer.reshape(count, width), qkv, edges, state_in, normed, tokens.reshape(count, width), weights, vectors,
+        two_sums, up_half, down_half, up_b, down_b,
     )
 
 
@@ -1507,10 +1602,10 @@
     start = lax.axis_index("dp") * own
     packed = lax.dynamic_update_slice(jnp.zeros((16, width), LOW), packed, (0, start))
     (
-        mixed, normed, qkv, edges, state_in, mixer, resid_grad, weights, vectors, two_sums, up_half, down_half,
+        mixed, normed, qkv, edges, state_in, mixer, resid_grad, weights, vectors, two_sums, up_half, down_half, up_b, down_b,
     ) = front(packed, qkv_weight, out_weight, up_weight, down_weight, tokens, out_grad, lengths)
     input_grad, up_sum, down_sum, out_sum, qkv_sum, small = back(
-        resid_grad, mixer, qkv, edges, state_in, normed, tokens, weights, vectors, two_sums, up_half, down_half,
+        resid_grad, mixer, qkv, edges, state_in, normed, tokens, weights, vectors, two_sums, up_half, down_half, up_b, down_b,
     )
     small = lax.dynamic_slice(small, (0, start), (16, own))
     return (

time: 221 us -> 212 us (0.959)
  Pallas kernels: 207 us -> 196 us
    pallas_call x1, Pallas kernels: 96.4 us -> 86.9 us  [back(): pl.pallas_call(back_kernel, out_shape=outs, in_specs=[anywhere] * 9 + [vm...]
where the time goes in v3:
time: 212 us; the launch traced here: 210 us
  Pallas kernels  196 us (92%)
  local copies, waits for them, and re-layouts  12.6 us (6%)
    pallas_call x1, Pallas kernels, front(): pl.pallas_call(front_kernel, out_shape=outs, in_specs=[pl.BlockSpec(memor...  109 us
    pallas_call x1, Pallas kernels, back(): pl.pallas_call(back_kernel, out_shape=outs, in_specs=[anywhere] * 9 + [vm...  86.9 us
    unnamed x18, local copies, waits for them, and re-layouts  8.14 us

profile of v3, /device:TPU:0, one launch (start us, length us, event | category | flops | bytes accessed | tf_op | source)
XLA Modules:
  0.0 209.7 jit_solution(349036774565690615)
XLA Ops:
  0.7 1.6 concatenate.3
  2.2 0.2 dynamic_update_slice.3.packed
  2.4 0.0 copy-start.5
  2.4 0.6 copy-done.5
  3.0 109.2 %gather_forward_ffn.1 = (bf16[2,512,768]{2,1,0:T(8,128)(2,1)}, bf16[1024,768]{1,0:T(8,128)(2,1)}, bf16[3,2,512,768]{3,2,1,0:T(8,128)(2,1)}, bf16[2,16,768]{2,1,0...) custom-call(s32[2]{0:T(128)} %lengths.1, ...), custom_call_target="tpu_custom_call" | custom-call | tf_op jit(solution)/shard_map/gather_forward_ffn/pallas_call | solution.py:715
  112.2 86.9 %backward_reduce.1 = (f32[2,512,768]{2,1,0:T(8,128)}, f32[48,3072]{1,0:T(8,128)}, f32[192,768]{1,0:T(8,128)}, f32[48,768]{1,0:T(8,128)}, f32[48,2304]{1,0:T(8,128)}, /*index=5*/f32[16,768]{1,0:T(8,128)}) custom-call(f32[2,512,768]{2,1,0:T(8,128)} %get-tuple-element.33.resid_grad_in, bf16[1024,768]{1,0:T(8,128)(2,1)} %bitcast.19, ...), custom_call_target="tpu_custom_call" | custom-call | tf_op jit(solution)/shard_map/backward_reduce/pallas_call | solution.py:1275
  199.1 1.4 dynamic-slice_bitcast_fusion
  200.6 1.3 dynamic-slice.2
  201.9 0.0 copy-start
  201.9 2.8 %copy.32 = bf16[2,512,768]{2,1,0:T(8,128)(2,1)} copy(bf16[2,512,768]{2,1,0:T(8,128)(2,1)} %get-tuple-element.69) | data formatting | bytes 3145728
  204.7 0.0 copy-done
  204.7 0.0 copy-start.3
  204.7 0.0 copy-start.4
  204.7 1.7 copy.33
  206.4 0.0 copy-done.3
  206.4 0.0 copy-start.2
  206.4 0.0 copy-start.1
  206.4 0.8 copy.34
  207.2 0.0 copy-done.4
  207.2 0.7 copy.35
  207.8 0.0 copy-done.2
  207.8 0.8 copy.36
  208.6 0.0 copy-done.1
  208.6 0.8 copy.37
  (2 shorter events, 0.0 us)
Async XLA Ops:
  2.4 0.6 copy-start.5
  201.9 2.8 %copy-start = (f32[2,512,768]{2,1,0:T(8,128)S(1)}, f32[2,512,768]{2,1,0:T(8,128)}, u32[]{:S(2)}) copy-start(f32[2,512,768]{2,1,0:T(8,128)} %get-tuple-element.70) | copy-start | bytes 9437188
  204.7 1.7 copy-start.3
  204.7 2.4 %copy-start.4 = (f32[48,768]{1,0:T(8,128)S(1)}, f32[48,768]{1,0:T(8,128)}, u32[]{:S(2)}) copy-start(f32[48,768]{1,0:T(8,128)} %get-tuple-element.76) | copy-start | bytes 442372
  206.4 1.4 copy-start.2
  206.4 2.2 %copy-start.1 = (f32[192,768]{1,0:T(8,128)S(1)}, f32[192,768]{1,0:T(8,128)}, u32[]{:S(2)}) copy-start(f32[192,768]{1,0:T(8,128)} %get-tuple-element.80) | copy-start | bytes 1769476
